TPU v7x, 32 devices: a whole 2x2x4 slice. The times are simulated.
32 devices in a mesh: dp: 4 (over y, core), seq: 8 (over z, x).
Axes of the slice: x: 2, y: 2, z: 4, core: 2. Of those that a mesh axis runs over, the one named last changes fastest.
Arguments:
- layer_input: bfloat16 [2, 4, 1024, 768], P(None, 'dp', 'seq'), may hold values from -6 to 6
- cotangent: bfloat16 [2, 4, 1024, 768], P(None, 'dp', 'seq'), may hold values from -6 to 6
- w_joined: bfloat16 [768, 2304], P(('dp', 'seq')), may hold values from -3 to 3
- w_output: bfloat16 [768, 768], P(('dp', 'seq')), may hold values from -2.5 to 2.5
- w_expand: bfloat16 [768, 2304], P(('dp', 'seq')), may hold values from -0.21875 to 0.21875
- w_contract: bfloat16 [1152, 768], P(None, ('dp', 'seq')), may hold values from -0.1875 to 0.1875
- gain_one: bfloat16 [768], P(('dp', 'seq')), may hold values from 0.5 to 1.5
- gain_two: bfloat16 [768], P(('dp', 'seq')), may hold values from 0.5 to 1.5
Outputs:
- layer_output: bfloat16 [2, 4, 1024, 768], P(None, 'dp', 'seq')
- input_grad: bfloat16 [2, 4, 1024, 768], P(None, 'dp', 'seq')
- w_joined_grad: float32 [768, 2304], P(('dp', 'seq'))
- w_output_grad: float32 [768, 768], P(('dp', 'seq'))
- w_expand_grad: float32 [768, 2304], P(('dp', 'seq'))
- w_contract_grad: float32 [1152, 768], P(None, ('dp', 'seq'))
- gain_one_grad: float32 [768], P(('dp', 'seq'))
- gain_two_grad: float32 [768], P(('dp', 'seq'))
All inputs are finite; a program needn't handle non-finite values.
Results may differ from a plain program's by a relative error of at most 0.02.
The roundings to bfloat16 on the way count: a program that leaves them out, or rounds other values in their place, can miss the bound.
Values may be sent and summed in bfloat16 or wider, within the bound.
A program may use at most 128 MiB of HBM per device.

v0:
```python
import jax
import jax.numpy as jnp
from jax import lax
from jax.sharding import PartitionSpec as P

HEADS = 12
HEAD_DIM = 64
WINDOW = 128


NORM_EPS = 1e-05
ROPE_BASE = 10000.0
MASK_FILL = -1e30
SQRT_HALF = 0.7071067811865476
INV_ROOT_TAU = 0.3989422804014327


def extended_2(value, sides, width):
    for axis, dim in sides:
        size, length = (lax.axis_size(axis), value.shape[dim])
        up = [(i, (i + 1) % size) for i in range(size - 1)]
        down = [(j, i) for i, j in up]
        last = lax.slice_in_dim(value, length - width, length, axis=dim)
        first = lax.slice_in_dim(value, 0, width, axis=dim)
        before = lax.ppermute(last, axis, up)
        after = lax.ppermute(first, axis, down)
        value = jnp.concatenate([before, value, after], axis=dim)
    return value


def norm_apply(values, gain):
    center = jnp.mean(values, axis=-1, keepdims=True)
    shifted = values - center
    inv_std = lax.rsqrt(jnp.mean(shifted * shifted, axis=-1, keepdims=True) + NORM_EPS)
    normed = shifted * inv_std
    return (normed * gain.astype(jnp.float32), normed, inv_std)


def norm_back(upstream, normed, inv_std, gain):
    scaled = upstream * gain.astype(jnp.float32)
    inner = (
        scaled
        - jnp.mean(scaled, axis=-1, keepdims=True)
        - normed * jnp.mean(scaled * normed, axis=-1, keepdims=True)
    )
    return (inv_std * inner, jnp.sum(upstream * normed, axis=(0, 1)))


def gelu_slope(values):
    cumul = 0.5 * (1.0 + jax.scipy.special.erf(values * SQRT_HALF))
    return cumul + values * jnp.exp(-0.5 * values * values) * INV_ROOT_TAU


def rope_tables(positions, head_dim):
    half_dim = head_dim // 2
    freqs = ROPE_BASE ** (-jnp.arange(half_dim).astype(jnp.float32) * 2.0 / head_dim)
    angles = positions.astype(jnp.float32)[:, None] * freqs[None, :]
    return (jnp.cos(angles)[:, None, :], jnp.sin(angles)[:, None, :])


def rotate(values, cosine, sine):
    half_dim = values.shape[-1] // 2
    first = values[..., :half_dim]
    second = values[..., half_dim:]
    return jnp.concatenate(
        [first * cosine - second * sine, second * cosine + first * sine], axis=-1
    )


def unrotate(values, cosine, sine):
    half_dim = values.shape[-1] // 2
    first = values[..., :half_dim]
    second = values[..., half_dim:]
    return jnp.concatenate(
        [first * cosine + second * sine, second * cosine - first * sine], axis=-1
    )


def per_device(
    layer_input, cotangent, w_joined, w_output, w_expand, w_contract, gain_one, gain_two
):
    micro, local_batch, group, width = layer_input.shape
    heads = HEADS
    head_dim = HEAD_DIM
    half = WINDOW // 2
    ffn = w_contract.shape[0]
    scale = head_dim ** (-0.5)
    seq_count = lax.axis_size("seq")
    group_start = lax.axis_index("seq") * group
    cosine, sine = rope_tables(group_start + jnp.arange(group, dtype=jnp.int32), head_dim)
    query_pos = group_start + jnp.arange(group, dtype=jnp.int32)[:, None]
    key_pos = group_start - half + jnp.arange(group + 2 * half, dtype=jnp.int32)[None, :]
    allowed = (
        (jnp.abs(query_pos - key_pos) <= half) & (key_pos >= 0) & (key_pos < group * seq_count)
    )
    contract_rows = w_contract.T
    gain_one_acc = jnp.zeros((width,), jnp.float32)
    gain_two_acc = jnp.zeros((width,), jnp.float32)
    outputs = []
    input_grads = []
    saved_normed_one = []
    saved_d_joined = []
    saved_normed_two = []
    saved_d_expanded = []
    saved_mixed = []
    saved_attended = []
    saved_d_resid = []
    for micro_index in range(micro):
        forward_set = (
            lax.all_gather(w_joined, ("dp", "seq"), axis=0, tiled=True),
            lax.all_gather(w_output, ("dp", "seq"), axis=0, tiled=True),
            lax.all_gather(w_expand, ("dp", "seq"), axis=0, tiled=True),
            lax.all_gather(contract_rows, ("dp", "seq"), axis=0, tiled=True),
            lax.all_gather(gain_one, ("dp", "seq"), axis=0, tiled=True),
            lax.all_gather(gain_two, ("dp", "seq"), axis=0, tiled=True),
        )
        full_joined, full_output, full_expand, full_contract, full_gain_one, full_gain_two = (
            forward_set
        )
        source32 = layer_input[micro_index].astype(jnp.float32)
        normed_f, norm_one, inv_one = norm_apply(source32, full_gain_one)
        normed_one = normed_f.astype(jnp.bfloat16)
        joined = jnp.einsum(
            "bcd,de->bce", normed_one, full_joined, preferred_element_type=jnp.float32
        )
        shape_heads = (local_batch, group, heads, head_dim)
        q_rot = rotate(joined[..., :width].reshape(shape_heads), cosine, sine).astype(jnp.bfloat16)
        k_rot = rotate(joined[..., width : 2 * width].reshape(shape_heads), cosine, sine).astype(
            jnp.bfloat16
        )
        v_half = joined[..., 2 * width :].astype(jnp.bfloat16)
        key_value = jnp.stack([k_rot.reshape(local_batch, group, width), v_half])
        extended = extended_2(key_value, (("seq", 2),), half)
        ext_shape = (local_batch, group + 2 * half, heads, head_dim)
        key_rows = extended[0].reshape(ext_shape)
        value_rows = extended[1].reshape(ext_shape)
        scores = (
            jnp.einsum("bqhd,bkhd->bhqk", q_rot, key_rows, preferred_element_type=jnp.float32)
            * scale
        )
        scores = jnp.where(allowed[None, None], scores, MASK_FILL)
        row_max = jnp.max(scores, axis=-1, keepdims=True)
        log_total = row_max + jnp.log(jnp.sum(jnp.exp(scores - row_max), axis=-1, keepdims=True))
        probs = jnp.exp(scores - log_total)
        probs_half = probs.astype(jnp.bfloat16)
        attended = jnp.einsum(
            "bhqk,bkhd->bqhd", probs_half, value_rows, preferred_element_type=jnp.float32
        )
        attended = attended.astype(jnp.bfloat16).reshape(local_batch, group, width)
        resid = source32 + jnp.einsum(
            "bcd,de->bce", attended, full_output, preferred_element_type=jnp.float32
        )
        normed_g, norm_two, inv_two = norm_apply(resid, full_gain_two)
        normed_two = normed_g.astype(jnp.bfloat16)
        expanded = jnp.einsum(
            "bcd,de->bce", normed_two, full_expand, preferred_element_type=jnp.float32
        )
        pre_act = expanded[..., :ffn]
        gate_part = expanded[..., ffn:]
        activated = jax.nn.gelu(pre_act, approximate=False)
        mixed = (activated * gate_part).astype(jnp.bfloat16)
        final = resid + jnp.einsum(
            "bcf,df->bcd", mixed, full_contract, preferred_element_type=jnp.float32
        )
        outputs.append(final.astype(jnp.bfloat16))
        backward_set = (
            lax.all_gather(w_joined, ("dp", "seq"), axis=0, tiled=True),
            lax.all_gather(w_output, ("dp", "seq"), axis=0, tiled=True),
            lax.all_gather(w_expand, ("dp", "seq"), axis=0, tiled=True),
            lax.all_gather(contract_rows, ("dp", "seq"), axis=0, tiled=True),
            lax.all_gather(gain_one, ("dp", "seq"), axis=0, tiled=True),
            lax.all_gather(gain_two, ("dp", "seq"), axis=0, tiled=True),
        )
        back_joined, back_output, back_expand, back_contract, back_gain_one, back_gain_two = (
            backward_set
        )
        upstream_half = cotangent[micro_index]
        d_mixed = jnp.einsum(
            "bcd,df->bcf", upstream_half, back_contract, preferred_element_type=jnp.float32
        )
        d_expanded = jnp.concatenate(
            [d_mixed * gate_part * gelu_slope(pre_act), d_mixed * activated], axis=-1
        ).astype(jnp.bfloat16)
        d_normed_two = jnp.einsum(
            "bce,de->bcd", d_expanded, back_expand, preferred_element_type=jnp.float32
        )
        d_resid_n, gain_two_part = norm_back(d_normed_two, norm_two, inv_two, back_gain_two)
        gain_two_acc = gain_two_acc + gain_two_part
        d_resid = upstream_half.astype(jnp.float32) + d_resid_n
        d_resid_half = d_resid.astype(jnp.bfloat16)
        d_attended = jnp.einsum(
            "bce,de->bcd", d_resid_half, back_output, preferred_element_type=jnp.float32
        )
        d_attended = d_attended.astype(jnp.bfloat16).reshape(shape_heads)
        d_probs = jnp.einsum(
            "bqhd,bkhd->bhqk", d_attended, value_rows, preferred_element_type=jnp.float32
        )
        centred = d_probs - jnp.sum(probs * d_probs, axis=-1, keepdims=True)
        d_scores = (probs * centred * scale).astype(jnp.bfloat16)
        d_query = jnp.einsum(
            "bhqk,bkhd->bqhd", d_scores, key_rows, preferred_element_type=jnp.float32
        )
        d_key_ext = jnp.einsum(
            "bhqk,bqhd->bkhd", d_scores, q_rot, preferred_element_type=jnp.float32
        )
        d_value_ext = jnp.einsum(
            "bhqk,bqhd->bkhd", probs_half, d_attended, preferred_element_type=jnp.float32
        )
        ext_grads = jnp.stack(
            [
                d_key_ext.reshape(local_batch, group + 2 * half, width),
                d_value_ext.reshape(local_batch, group + 2 * half, width),
            ]
        )
        rim_grads = jnp.concatenate(
            [ext_grads[:, :, :half], ext_grads[:, :, group + half :]], axis=2
        )
        returned = extended_2(rim_grads.astype(jnp.bfloat16), (("seq", 2),), half).astype(
            rim_grads.dtype
        )
        own_grads = ext_grads[:, :, half : half + group]
        own_grads = own_grads.at[:, :, :half].add(returned[:, :, :half])
        own_grads = own_grads.at[:, :, group - half :].add(returned[:, :, 3 * half :])
        d_key = unrotate(own_grads[0].reshape(shape_heads), cosine, sine).reshape(
            local_batch, group, width
        )
        d_query_flat = unrotate(d_query, cosine, sine).reshape(local_batch, group, width)
        d_joined = jnp.concatenate([d_query_flat, d_key, own_grads[1]], axis=-1).astype(
            jnp.bfloat16
        )
        d_normed_one = jnp.einsum(
            "bce,de->bcd", d_joined, back_joined, preferred_element_type=jnp.float32
        )
        d_source, gain_one_part = norm_back(d_normed_one, norm_one, inv_one, back_gain_one)
        gain_one_acc = gain_one_acc + gain_one_part
        input_grads.append((d_resid + d_source).astype(jnp.bfloat16))
        saved_normed_one.append(normed_one)
        saved_d_joined.append(d_joined)
        saved_normed_two.append(normed_two)
        saved_d_expanded.append(d_expanded)
        saved_mixed.append(mixed)
        saved_attended.append(attended)
        saved_d_resid.append(d_resid_half)
    joined_acc = jnp.einsum(
        "mbcd,mbce->de",
        jnp.stack(saved_normed_one),
        jnp.stack(saved_d_joined),
        preferred_element_type=jnp.float32,
    )
    output_acc = jnp.einsum(
        "mbcd,mbce->de",
        jnp.stack(saved_attended),
        jnp.stack(saved_d_resid),
        preferred_element_type=jnp.float32,
    )
    expand_acc = jnp.einsum(
        "mbcd,mbce->de",
        jnp.stack(saved_normed_two),
        jnp.stack(saved_d_expanded),
        preferred_element_type=jnp.float32,
    )
    contract_acc = jnp.einsum(
        "mbcd,mbcf->df", cotangent, jnp.stack(saved_mixed), preferred_element_type=jnp.float32
    )
    summed = (
        lax.psum_scatter(joined_acc, ("dp", "seq"), scatter_dimension=0, tiled=True),
        lax.psum_scatter(output_acc, ("dp", "seq"), scatter_dimension=0, tiled=True),
        lax.psum_scatter(expand_acc, ("dp", "seq"), scatter_dimension=0, tiled=True),
        lax.psum_scatter(contract_acc, ("dp", "seq"), scatter_dimension=0, tiled=True),
        lax.psum_scatter(gain_one_acc, ("dp", "seq"), scatter_dimension=0, tiled=True),
        lax.psum_scatter(gain_two_acc, ("dp", "seq"), scatter_dimension=0, tiled=True),
    )
    return (
        jnp.stack(outputs),
        jnp.stack(input_grads),
        summed[0],
        summed[1],
        summed[2],
        summed[3].T,
        summed[4],
        summed[5],
    )


def solution(mesh):
    placed = (
        P(None, "dp", "seq", None),
        P(None, "dp", "seq", None),
        P(("dp", "seq"), None),
        P(("dp", "seq"), None),
        P(("dp", "seq"), None),
        P(None, ("dp", "seq")),
        P(("dp", "seq")),
        P(("dp", "seq")),
    )
    return jax.shard_map(
        per_device,
        mesh=mesh,
        in_specs=placed,
        out_specs=(
            P(None, "dp", "seq", None),
            P(None, "dp", "seq", None),
            P(("dp", "seq"), None),
            P(("dp", "seq"), None),
            P(("dp", "seq"), None),
            P(None, ("dp", "seq")),
            P(("dp", "seq")),
            P(("dp", "seq")),
        ),
        check_vma=False,
    )
```

profile of v0, /device:TPU:0, one launch (start us, length us, event | category | flops | bytes accessed | tf_op | source)
XLA Modules:
  0.0 772.4 jit_solution(8772358290523111538)
XLA Ops:
  11.8 42.1 %all-reduce.6 = (bf16[768]{0:T(1024)(128)(2,1)S(1)}, bf16[768]{0:T(1024)(128)(2,1)S(1)}) all-reduce(bf16[768]{0:T(1024)(128)(2,1)S(1)} %dynamic-update-slice.12, bf16[768]{0:T(1024)(128)(2,1)S(1)} %dynamic-update-slice.13), channel_id=1, replica_groups=mesh['dp'=4,'seq'=8] {'dp','seq'}, use_global_device_ids=true, to_apply=%add | all-reduce | flops 1536 | bytes 6144
  58.5 15.5 %all-gather.5.cloned.1.call-done = bf16[768,2304]{1,0:T(8,128)(2,1)} async-done(((bf16[24,2304]{1,0:T(8,128)(2,1)}), bf16[768,2304]{1,0:T(8,128)(2,1)}) %all-gather.5.cloned.1.call-update) | async-done | bytes 3538960 | tf_op jit(solution)/shard_map/all_gather | solution.py:110
  74.0 2.8 convolution_bitcast_fusion.6
  77.9 2.7 convolution_bitcast_fusion.4
  82.7 1.9 copy.96
  84.6 1.9 copy.88
  86.5 2.2 fusion.203
  91.0 4.6 collective-permute-start.2
  97.7 5.0 collective-permute-start
  102.8 5.6 collective-permute-done.2
  111.6 23.3 %all-gather.7.cloned.1.call-done = bf16[768,768]{1,0:T(8,128)(2,1)} async-done(((bf16[24,768]{1,0:T(8,128)(2,1)}), bf16[768,768]{1,0:T(8,128)(2,1)}) %all-gather.7.cloned.1.call-update) | async-done | bytes 1179664 | tf_op jit(solution)/shard_map/all_gather | solution.py:111
  136.9 60.0 %all-gather.9.cloned.1.call-done = bf16[768,2304]{1,0:T(8,128)(2,1)} async-done(((bf16[24,2304]{1,0:T(8,128)(2,1)}), bf16[768,2304]{1,0:T(8,128)(2,1)}) %all-gather.9.cloned.1.call-update) | async-done | bytes 3538960 | tf_op jit(solution)/shard_map/all_gather | solution.py:112
  196.8 2.7 convolution_bitcast_fusion.3
  199.6 54.4 %all-gather.11.cloned.1.call-done = bf16[768,1152]{1,0:T(8,128)(2,1)} async-done(((bf16[24,1152]{1,0:T(8,128)(2,1)}), bf16[768,1152]{1,0:T(8,128)(2,1)}) %all-gather.11.cloned.1.call-update) | async-done | bytes 1769488 | tf_op jit(solution)/shard_map/all_gather | solution.py:113
  254.0 4.1 multiply_convert_fusion.2
  265.3 2.6 multiply_convert_fusion.3
  268.9 2.5 convolution_bitcast_fusion.2
  271.7 2.4 fusion.78
  277.7 1.9 convolution_bitcast_fusion.9
  280.8 3.9 convolution_bitcast_fusion
  288.0 1.9 copy.104
  289.9 2.7 fusion.247
  292.5 11.3 %fusion.15 = f32[12,64,256]{2,1,0:T(8,128)} fusion(f32[12,128,256]{2,1,0:T(8,128)} %fusion.247, f32[12,128,256]{2,1,0:T(8,128)S(1)} %copy-done.2, f32[12,128]{1,0:T(8,128)} %copy-done.82, bf16[128,12,32]{0,2,1:T(8,128)(2,1)} %get-tuple-element.160, bf16[128,12,32]{0,2,1:T(8,128)(2,1)} %get-tuple-element.161), kind=kOutput, calls=%fused_computation.38 | convolution fusion | flops 53479168 | bytes 4134912 | tf_op jit(solution)/shard_map/bhqk,bqhd->bkhd/dot_general | solution.py:203
  303.8 2.4 copy.105
  306.2 2.3 fusion.177
  308.5 2.3 copy.106
  310.8 2.0 fusion.153
  314.1 5.2 collective-permute-start.6
  320.6 1.9 copy.98
  322.4 2.7 fusion.246
  325.1 11.4 %fusion.9 = f32[12,64,256]{2,1,0:T(8,128)} fusion(f32[12,128,256]{2,1,0:T(8,128)} %fusion.246, f32[12,128,256]{2,1,0:T(8,128)S(1)} %copy-done.4, f32[12,128]{1,0:T(8,128)} %copy-done.83, bf16[128,12,32]{0,2,1:T(8,128)(2,1)} %get-tuple-element.133, bf16[128,12,32]{0,2,1:T(8,128)(2,1)} %get-tuple-element.132), kind=kOutput, calls=%fused_computation.36 | convolution fusion | flops 53479168 | bytes 4134912 | tf_op jit(solution)/shard_map/bhqk,bqhd->bkhd/dot_general | solution.py:203
  336.5 2.3 copy.99
  338.8 2.3 fusion.180
  341.2 2.4 copy.100
  343.5 2.1 fusion.158
  347.0 5.5 collective-permute-start.4
  352.5 1.9 maximum_bitcast_fusion.7
  356.3 11.3 %fusion.23 = f32[1,128,12,64]{1,3,2,0:T(8,128)} fusion(bf16[256,12,64]{0,2,1:T(8,128)(2,1)} %bitcast.334, f32[12,128,256]{2,1,0:T(8,128)} %fusion.246, f32[12,128,256]{2,1,0:T(8,128)S(1)} %copy-done.4, f32[12,128]{1,0:T(8,128)} %copy-done.83), kind=kOutput, calls=%fused_computation.41 | convolution fusion | flops 53085952 | bytes 3938304 | tf_op jit(solution)/shard_map/bhqk,bkhd->bqhd/dot_general | solution.py:200
  367.6 1.9 maximum_bitcast_fusion.6
  369.5 11.2 %fusion.20 = f32[1,128,12,64]{1,3,2,0:T(8,128)} fusion(bf16[256,12,64]{0,2,1:T(8,128)(2,1)} %bitcast.332, f32[12,128,256]{2,1,0:T(8,128)} %fusion.247, f32[12,128,256]{2,1,0:T(8,128)S(1)} %copy-done.2, f32[12,128]{1,0:T(8,128)} %copy-done.82), kind=kOutput, calls=%fused_computation.40 | convolution fusion | flops 53085952 | bytes 3938304 | tf_op jit(solution)/shard_map/bhqk,bkhd->bqhd/dot_general | solution.py:200
  380.8 1.7 fusion.156
  382.5 2.0 fusion.162
  391.5 4.0 convolution_bitcast_fusion.1
  402.1 3.5 fusion.92
  407.1 39.2 %all-reduce.5 = (f32[768]{0:T(1024)S(1)}, f32[768]{0:T(1024)S(1)}) all-reduce(f32[768]{0:T(1024)S(1)} %add.230, f32[768]{0:T(1024)S(1)} %add.231), channel_id=6, replica_groups=mesh['dp'=4,'seq'=8] {'dp','seq'}, use_global_device_ids=true, to_apply=%region_28.29.clone | all-reduce | flops 1536 | bytes 12288
  451.0 64.5 %reduce-scatter.7.cloned.1.call-done = f32[24,768]{1,0:T(8,128)} async-done(((f32[768,768]{1,0:T(8,128)}), f32[24,768]{1,0:T(8,128)}) %reduce-scatter.7.cloned.1.call-update) | async-done | bytes 73744 | tf_op jit(solution)/shard_map/reduce_scatter | solution.py:267
  515.5 124.8 %reduce-scatter.9.cloned.1.call-done = f32[24,2304]{1,0:T(8,128)} async-done(((f32[768,2304]{1,0:T(8,128)}), f32[24,2304]{1,0:T(8,128)}) %reduce-scatter.9.cloned.1.call-update) | async-done | bytes 221200 | tf_op jit(solution)/shard_map/reduce_scatter | solution.py:268
  640.3 124.8 %reduce-scatter.5.cloned.1.call-done = f32[24,2304]{1,0:T(8,128)} async-done(((f32[768,2304]{1,0:T(8,128)}), f32[24,2304]{1,0:T(8,128)}) %reduce-scatter.5.cloned.1.call-update) | async-done | bytes 221200 | tf_op jit(solution)/shard_map/reduce_scatter | solution.py:266
  (347 shorter events, 62.5 us)
Async XLA Ops:
  7.2 66.8 %all-gather.5.cloned.1.call-start = ((), (), s32[]{:S(2)}) async-start(), calls=%async_computation.3 | async-start | bytes 3649536 | tf_op jit(solution)/shard_map/all_gather | solution.py:110
  7.9 127.0 %all-gather.7.cloned.1.call-start = ((), (), s32[]{:S(2)}) async-start(), calls=%async_computation.4 | async-start | bytes 1216512 | tf_op jit(solution)/shard_map/all_gather | solution.py:111
  8.6 188.2 %all-gather.9.cloned.1.call-start = ((), (), s32[]{:S(2)}) async-start(), calls=%async_computation.5 | async-start | bytes 3649536 | tf_op jit(solution)/shard_map/all_gather | solution.py:112
  9.4 244.6 %all-gather.11.cloned.1.call-start = ((), (), s32[]{:S(2)}) async-start(), calls=%async_computation.6 | async-start | bytes 1824768 | tf_op jit(solution)/shard_map/all_gather | solution.py:113
  10.0 438.7 %all-reduce.9.cloned.1.call-start = ((), (), s32[]{:S(2)}) async-start(), calls=%async_computation.10 | async-start | bytes 7077888
  53.9 23.9 %copy-start.76 = (f32[768]{0:T(1024)}, f32[768]{0:T(1024)S(1)}, u32[]{:S(2)}) copy-start(f32[768]{0:T(1024)S(1)} %convert_element_type.324) | copy-start | bytes 9220
  55.1 21.7 %copy-start.89 = (f32[128]{0:T(128)}, f32[128]{0:T(128)S(1)}, u32[]{:S(2)}) copy-start(f32[128]{0:T(128)S(1)} %get-tuple-element.180) | copy-start | bytes 1540
  55.1 22.7 %copy-start.86 = (f32[128]{0:T(128)}, f32[128]{0:T(128)S(1)}, u32[]{:S(2)}) copy-start(f32[128]{0:T(128)S(1)} %get-tuple-element.179) | copy-start | bytes 1540
  56.4 20.4 %copy-start.96 = (f32[128]{0:T(128)}, f32[128]{0:T(128)S(1)}, u32[]{:S(2)}) copy-start(f32[128]{0:T(128)S(1)} %add_rsqrt_fusion.3) | copy-start | bytes 1540
  56.4 21.4 %copy-start.99 = (f32[128]{0:T(128)}, f32[128]{0:T(128)S(1)}, u32[]{:S(2)}) copy-start(f32[128]{0:T(128)S(1)} %add_rsqrt_fusion.1) | copy-start | bytes 1540
  88.7 6.9 copy-start.68
  88.7 6.9 copy-start.69
  89.7 13.1 %collective-permute-start.3 = (bf16[2,1,64,768]{3,2,1,0:T(8,128)(2,1)}, bf16[2,1,64,768]{3,2,1,0:T(8,128)(2,1)S(1)}, u32[]{:S(2)}, u32[]{:S(2)}) collective-permute-start(bf16[2,1,64,768]{3,2,1,0:T(8,128)(2,1)} %get-tuple-element.151), channel_id=1, source_target_pairs={{1,0},{2,1},{3,2},{4,3},{5,4},{6,5},{7,6},{9,8},{10,9},{11,10},{12... | collective-permute-start | bytes 589832 | tf_op jit(solution)/shard_map/ppermute | solution.py:26
  91.0 17.4 %collective-permute-start.2 = (bf16[2,1,64,768]{3,2,1,0:T(8,128)(2,1)}, bf16[2,1,64,768]{3,2,1,0:T(8,128)(2,1)S(1)}, u32[]{:S(2)}, u32[]{:S(2)}) collective-permute-start(bf16[2,1,64,768]{3,2,1,0:T(8,128)(2,1)} %get-tuple-element.150), channel_id=1, source_target_pairs={{0,1},{1,2},{2,3},{3,4},{4,5},{5,6},{6,7},{8,9},{9,10},{10,11},{11... | collective-permute-start | bytes 589832 | tf_op jit(solution)/shard_map/ppermute | solution.py:25
  96.5 162.4 %collective-permute-start.1 = (bf16[2,1,64,768]{3,2,1,0:T(8,128)(2,1)}, bf16[2,1,64,768]{3,2,1,0:T(8,128)(2,1)S(1)}, u32[]{:S(2)}, u32[]{:S(2)}) collective-permute-start(bf16[2,1,64,768]{3,2,1,0:T(8,128)(2,1)} %get-tuple-element.149), channel_id=1, source_target_pairs={{1,0},{2,1},{3,2},{4,3},{5,4},{6,5},{7,6},{9,8},{10,9},{11,10},{12... | collective-permute-start | bytes 589832 | tf_op jit(solution)/shard_map/ppermute | solution.py:26
  97.7 161.1 %collective-permute-start = (bf16[2,1,64,768]{3,2,1,0:T(8,128)(2,1)S(1)}, bf16[2,1,64,768]{3,2,1,0:T(8,128)(2,1)S(1)}, u32[]{:S(2)}, u32[]{:S(2)}) collective-permute-start(bf16[2,1,64,768]{3,2,1,0:T(8,128)(2,1)S(1)} %get-tuple-element.148), channel_id=1, source_target_pairs={{0,1},{1,2},{2,3},{3,4},{4,5},{5,6},{6,7},{8,9},{9,10},{10,11},{11... | collective-permute-start | bytes 589832 | tf_op jit(solution)/shard_map/ppermute | solution.py:25
  110.5 26.1 %copy-start.82 = (f32[12,128]{1,0:T(8,128)}, f32[12,128]{1,0:T(8,128)S(1)}, u32[]{:S(2)}) copy-start(f32[12,128]{1,0:T(8,128)S(1)} %log_add_fusion) | copy-start | bytes 18436
  111.6 25.3 %copy-start.41 = (bf16[12,64,128]{2,1,0:T(8,128)(2,1)}, bf16[12,64,128]{2,1,0:T(8,128)(2,1)S(1)}, u32[]{:S(2)}) copy-start(bf16[12,64,128]{2,1,0:T(8,128)(2,1)S(1)} %convolution_convert_fusion.2) | copy-start | bytes 589828
  111.6 85.3 %copy-start.79 = (f32[768]{0:T(1024)S(1)}, f32[768]{0:T(1024)}, u32[]{:S(2)}) copy-start(f32[768]{0:T(1024)} %convert_element_type.333) | copy-start | bytes 9220
  136.6 62.9 %copy-start.11 = (f32[128,768]{1,0:T(8,128)}, f32[128,768]{1,0:T(8,128)S(1)}, u32[]{:S(2)}) copy-start(f32[128,768]{1,0:T(8,128)S(1)} %get-tuple-element.173) | copy-start | bytes 1179652
  136.6 62.9 %copy-start.92 = (f32[128]{0:T(128)}, f32[128]{0:T(128)S(1)}, u32[]{:S(2)}) copy-start(f32[128]{0:T(128)S(1)} %broadcast_multiply_fusion.8) | copy-start | bytes 1540
  136.8 62.7 %copy-start.102 = (f32[128]{0:T(128)}, f32[128]{0:T(128)S(1)}, u32[]{:S(2)}) copy-start(f32[128]{0:T(128)S(1)} %add_rsqrt_fusion) | copy-start | bytes 1540
  136.9 117.1 %copy-start.53 = (bf16[2,1,128,768]{3,2,1,0:T(8,128)(2,1)S(1)}, bf16[2,1,128,768]{3,2,1,0:T(8,128)(2,1)}, u32[]{:S(2)}) copy-start(bf16[2,1,128,768]{3,2,1,0:T(8,128)(2,1)} %param.17) | copy-start | bytes 1179652
  271.5 244.1 %reduce-scatter.7.cloned.1.call-start = ((), (), s32[]{:S(2)}) async-start(), calls=%async_computation.8 | async-start | bytes 2433024 | tf_op jit(solution)/shard_map/reduce_scatter | solution.py:267
  277.0 9.8 %copy-start.31 = (f32[128,768]{1,0:T(8,128)}, f32[128,768]{1,0:T(8,128)S(1)}, u32[]{:S(2)}) copy-start(f32[128,768]{1,0:T(8,128)S(1)} %get-tuple-element.147) | copy-start | bytes 1179652
  277.0 42.4 %copy-start.29 = (f32[128,768]{1,0:T(8,128)}, f32[128,768]{1,0:T(8,128)S(1)}, u32[]{:S(2)}) copy-start(f32[128,768]{1,0:T(8,128)S(1)} %get-tuple-element.103) | copy-start | bytes 1179652
  279.6 360.7 %reduce-scatter.9.cloned.1.call-start = ((), (), s32[]{:S(2)}) async-start(), calls=%async_computation.9 | async-start | bytes 7299072 | tf_op jit(solution)/shard_map/reduce_scatter | solution.py:268
  284.8 480.3 %reduce-scatter.5.cloned.1.call-start = ((), (), s32[]{:S(2)}) async-start(), calls=%async_computation.7 | async-start | bytes 7299072 | tf_op jit(solution)/shard_map/reduce_scatter | solution.py:266
  288.0 4.5 copy-start.2
  312.8 67.9 %collective-permute-start.7 = (bf16[2,1,64,768]{3,2,0,1:T(8,128)(2,1)}, bf16[2,1,64,768]{3,2,0,1:T(8,128)(2,1)}, u32[]{:S(2)}, u32[]{:S(2)}) collective-permute-start(bf16[2,1,64,768]{3,2,0,1:T(8,128)(2,1)} %get-tuple-element.115), channel_id=1, source_target_pairs={{1,0},{2,1},{3,2},{4,3},{5,4},{6,5},{7,6},{9,8},{10,9},{11,10},{12... | collective-permute-start | bytes 589832 | tf_op jit(solution)/shard_map/ppermute | solution.py:26
  314.1 66.6 %collective-permute-start.6 = (bf16[2,1,64,768]{3,2,0,1:T(8,128)(2,1)}, bf16[2,1,64,768]{3,2,0,1:T(8,128)(2,1)}, u32[]{:S(2)}, u32[]{:S(2)}) collective-permute-start(bf16[2,1,64,768]{3,2,0,1:T(8,128)(2,1)} %get-tuple-element.114), channel_id=1, source_target_pairs={{0,1},{1,2},{2,3},{3,4},{4,5},{5,6},{6,7},{8,9},{9,10},{10,11},{11... | collective-permute-start | bytes 589832 | tf_op jit(solution)/shard_map/ppermute | solution.py:25
  320.6 4.6 copy-start.4
  343.5 10.8 %copy-start.17 = (f32[1,1,256,768]{3,2,0,1:T(8,128)S(1)}, f32[1,1,256,768]{3,2,0,1:T(8,128)}, u32[]{:S(2)}) copy-start(f32[1,1,256,768]{3,2,0,1:T(8,128)} %copy.105) | copy-start | bytes 2359300
  343.5 10.8 %copy-start.19 = (f32[1,1,256,768]{3,2,0,1:T(8,128)S(1)}, f32[1,1,256,768]{3,2,0,1:T(8,128)}, u32[]{:S(2)}) copy-start(f32[1,1,256,768]{3,2,0,1:T(8,128)} %copy.106) | copy-start | bytes 2359300
  345.7 41.0 %collective-permute-start.5 = (bf16[2,1,64,768]{3,2,0,1:T(8,128)(2,1)}, bf16[2,1,64,768]{3,2,0,1:T(8,128)(2,1)}, u32[]{:S(2)}, u32[]{:S(2)}) collective-permute-start(bf16[2,1,64,768]{3,2,0,1:T(8,128)(2,1)} %get-tuple-element.113), channel_id=1, source_target_pairs={{1,0},{2,1},{3,2},{4,3},{5,4},{6,5},{7,6},{9,8},{10,9},{11,10},{12... | collective-permute-start | bytes 589832 | tf_op jit(solution)/shard_map/ppermute | solution.py:26
  347.0 39.7 %collective-permute-start.4 = (bf16[2,1,64,768]{3,2,0,1:T(8,128)(2,1)}, bf16[2,1,64,768]{3,2,0,1:T(8,128)(2,1)}, u32[]{:S(2)}, u32[]{:S(2)}) collective-permute-start(bf16[2,1,64,768]{3,2,0,1:T(8,128)(2,1)} %get-tuple-element.112), channel_id=1, source_target_pairs={{0,1},{1,2},{2,3},{3,4},{4,5},{5,6},{6,7},{8,9},{9,10},{10,11},{11... | collective-permute-start | bytes 589832 | tf_op jit(solution)/shard_map/ppermute | solution.py:25
  367.6 13.1 %copy-start.18 = (f32[1,1,256,768]{3,2,0,1:T(8,128)S(1)}, f32[1,1,256,768]{3,2,0,1:T(8,128)}, u32[]{:S(2)}) copy-start(f32[1,1,256,768]{3,2,0,1:T(8,128)} %copy.105) | copy-start | bytes 2359300
  367.6 13.2 %copy-start.20 = (f32[1,1,256,768]{3,2,0,1:T(8,128)S(1)}, f32[1,1,256,768]{3,2,0,1:T(8,128)}, u32[]{:S(2)}) copy-start(f32[1,1,256,768]{3,2,0,1:T(8,128)} %copy.106) | copy-start | bytes 2359300
  382.5 4.1 copy-start.22
  382.5 4.1 copy-start.24
  382.5 4.1 copy-start.27
  382.5 4.1 copy-start.33
  390.4 5.1 copy-start.45
  390.6 5.0 copy-start.47
  390.8 4.8 copy-start.49
  390.9 4.6 copy-start.51
  405.6 41.8 %copy-start.30 = (f32[128,768]{1,0:T(8,128)S(1)}, f32[128,768]{1,0:T(8,128)}, u32[]{:S(2)}) copy-start(f32[128,768]{1,0:T(8,128)} %copy-done.29) | copy-start | bytes 1179652
  405.7 41.8 %copy-start.32 = (f32[128,768]{1,0:T(8,128)S(1)}, f32[128,768]{1,0:T(8,128)}, u32[]{:S(2)}) copy-start(f32[128,768]{1,0:T(8,128)} %copy-done.31) | copy-start | bytes 1179652
  (74 other events, 114.7 us)
Sparse Core Ops, SparseCore 0:
  11.0 62.9 all-gather.4
  76.9 57.8 all-gather.6
  137.9 58.9 all-gather.8
  199.5 54.3 all-gather.10
  271.6 138.9 all-reduce.8
  416.2 99.2 reduce-scatter.6
  521.8 118.5 reduce-scatter.8
  646.6 118.4 reduce-scatter.4
where the time goes:
time: 778 us; the launch traced here: 772 us
  waiting for transfers between devices  476 us (61%)
  matrix products  99.6 us (13%)
  blocking collectives  81.3 us (10%)
  local copies, waits for them, and re-layouts  43 us (6%)
  other arithmetic  30.7 us (4%)
  starting transfers between devices  26 us (3%)
  between operations  16.2 us (2%)
    reduce_scatter x1, waiting for transfers between devices, per_device(): lax.psum_scatter(expand_acc, ('dp', 'seq'), scatter_dimension=0, tiled=True)  125 us
    reduce_scatter x1, waiting for transfers between devices, per_device(): lax.psum_scatter(joined_acc, ('dp', 'seq'), scatter_dimension=0, tiled=True)  125 us
    unnamed x2, blocking collectives  81.3 us
    reduce_scatter x1, waiting for transfers between devices, per_device(): lax.psum_scatter(output_acc, ('dp', 'seq'), scatter_dimension=0, tiled=True)  64.5 us
    all_gather x1, waiting for transfers between devices, per_device(): lax.all_gather(w_expand, ('dp', 'seq'), axis=0, tiled=True)  60 us
    all_gather x1, waiting for transfers between devices, per_device(): lax.all_gather(contract_rows, ('dp', 'seq'), axis=0, tiled=True)  54.4 us
    all_gather x1, waiting for transfers between devices, per_device(): lax.all_gather(w_output, ('dp', 'seq'), axis=0, tiled=True)  23.3 us
    dot_general x2, matrix products, per_device(): jnp.einsum('bhqk,bqhd->bkhd', d_scores, q_rot, preferred_element_type=jnp...  22.7 us
  transfers between devices with their start and end apart: 16, of which 8 were waited for; matrix products, arithmetic and copies ran while one was open for 20% of the time, Pallas kernels for 0%

commit v1 on v0

v1 whole, which is shorter than its diff:
```python
import jax
import jax.numpy as jnp
from jax import lax
from jax.sharding import PartitionSpec as P

HEADS = 12
HEAD_DIM = 64
WINDOW = 128


NORM_EPS = 1e-05
ROPE_BASE = 10000.0
MASK_FILL = -1e30
SQRT_HALF = 0.7071067811865476
INV_ROOT_TAU = 0.3989422804014327


LANES = 128


def scatter_sum(value, axes):
    value = value.astype(jnp.bfloat16)
    for axis in axes:
        size = lax.axis_size(axis)
        blocks = value.reshape(size, value.shape[0] // size, value.shape[1])
        value = jnp.sum(lax.all_to_all(blocks, axis, 0, 0).astype(jnp.float32), axis=0)
    return value


def norm_apply(values, gain):
    center = jnp.mean(values, axis=-1, keepdims=True)
    shifted = values - center
    inv_std = lax.rsqrt(jnp.mean(shifted * shifted, axis=-1, keepdims=True) + NORM_EPS)
    normed = shifted * inv_std
    return (normed * gain.astype(jnp.float32), normed, inv_std)


def norm_back(upstream, normed, inv_std, gain):
    scaled = upstream * gain.astype(jnp.float32)
    inner = (
        scaled
        - jnp.mean(scaled, axis=-1, keepdims=True)
        - normed * jnp.mean(scaled * normed, axis=-1, keepdims=True)
    )
    return (inv_std * inner, jnp.sum(upstream * normed, axis=(0, 1)))


def gelu_slope(values):
    cumul = 0.5 * (1.0 + jax.scipy.special.erf(values * SQRT_HALF))
    return cumul + values * jnp.exp(-0.5 * values * values) * INV_ROOT_TAU


def rope_tables(positions, head_dim):
    half_dim = head_dim // 2
    freqs = ROPE_BASE ** (-jnp.arange(half_dim).astype(jnp.float32) * 2.0 / head_dim)
    angles = positions.astype(jnp.float32)[:, None] * freqs[None, :]
    return (jnp.cos(angles)[:, None, :], jnp.sin(angles)[:, None, :])


def rotate(values, cosine, sine):
    half_dim = values.shape[-1] // 2
    first = values[..., :half_dim]
    second = values[..., half_dim:]
    return jnp.concatenate(
        [first * cosine - second * sine, second * cosine + first * sine], axis=-1
    )


def unrotate(values, cosine, sine):
    half_dim = values.shape[-1] // 2
    first = values[..., :half_dim]
    second = values[..., half_dim:]
    return jnp.concatenate(
        [first * cosine + second * sine, second * cosine - first * sine], axis=-1
    )


def per_device(
    layer_input, cotangent, w_joined, w_output, w_expand, w_contract, gain_one, gain_two
):
    micro, local_batch, group, width = layer_input.shape
    heads = HEADS
    head_dim = HEAD_DIM
    half = WINDOW // 2
    ffn = w_contract.shape[0]
    batch = micro * local_batch
    scale = head_dim ** (-0.5)
    axes = ("dp", "seq")
    seq_count = lax.axis_size("seq")
    up = [(i, i + 1) for i in range(seq_count - 1)]
    down = [(j, i) for i, j in up]
    group_start = lax.axis_index("seq") * group
    cosine, sine = rope_tables(group_start + jnp.arange(group, dtype=jnp.int32), head_dim)
    query_pos = group_start + jnp.arange(group, dtype=jnp.int32)[:, None]
    key_pos = group_start - half + jnp.arange(group + 2 * half, dtype=jnp.int32)[None, :]
    allowed = (
        (jnp.abs(query_pos - key_pos) <= half) & (key_pos >= 0) & (key_pos < group * seq_count)
    )
    gains = jnp.pad(jnp.stack([gain_one, gain_two], axis=1), ((0, 0), (0, LANES - 2)))
    pack_one = jnp.concatenate([w_joined, gains], axis=1)
    pack_two = jnp.concatenate([w_expand, w_contract.T, w_output], axis=1)
    full_one = lax.all_gather(pack_one, axes, axis=0, tiled=True)
    full_two = lax.all_gather(pack_two, axes, axis=0, tiled=True)
    full_joined = full_one[:, : 3 * width]
    full_gain_one = full_one[:, 3 * width]
    full_gain_two = full_one[:, 3 * width + 1]
    full_expand = full_two[:, : 2 * ffn]
    full_contract = full_two[:, 2 * ffn : 3 * ffn]
    full_output = full_two[:, 3 * ffn :]

    source32 = layer_input.reshape(batch, group, width).astype(jnp.float32)
    upstream_half = cotangent.reshape(batch, group, width)
    normed_f, norm_one, inv_one = norm_apply(source32, full_gain_one)
    normed_one = normed_f.astype(jnp.bfloat16)
    joined = jnp.einsum(
        "bcd,de->bce", normed_one, full_joined, preferred_element_type=jnp.float32
    )
    shape_heads = (batch, group, heads, head_dim)
    k_rot = rotate(joined[..., width : 2 * width].reshape(shape_heads), cosine, sine).astype(
        jnp.bfloat16
    )
    v_half = joined[..., 2 * width :].astype(jnp.bfloat16)
    key_value = jnp.stack([k_rot.reshape(batch, group, width), v_half])
    before = lax.ppermute(key_value[:, :, group - half :], "seq", up)
    after = lax.ppermute(key_value[:, :, :half], "seq", down)
    q_rot = rotate(joined[..., :width].reshape(shape_heads), cosine, sine).astype(jnp.bfloat16)
    extended = jnp.concatenate([before, key_value, after], axis=2)
    ext_shape = (batch, group + 2 * half, heads, head_dim)
    key_rows = extended[0].reshape(ext_shape)
    value_rows = extended[1].reshape(ext_shape)
    scores = (
        jnp.einsum("bqhd,bkhd->bhqk", q_rot, key_rows, preferred_element_type=jnp.float32)
        * scale
    )
    scores = jnp.where(allowed[None, None], scores, MASK_FILL)
    row_max = jnp.max(scores, axis=-1, keepdims=True)
    log_total = row_max + jnp.log(jnp.sum(jnp.exp(scores - row_max), axis=-1, keepdims=True))
    probs = jnp.exp(scores - log_total)
    probs_half = probs.astype(jnp.bfloat16)
    attended = jnp.einsum(
        "bhqk,bkhd->bqhd", probs_half, value_rows, preferred_element_type=jnp.float32
    )
    attended = attended.astype(jnp.bfloat16).reshape(batch, group, width)
    resid = source32 + jnp.einsum(
        "bcd,de->bce", attended, full_output, preferred_element_type=jnp.float32
    )
    normed_g, norm_two, inv_two = norm_apply(resid, full_gain_two)
    normed_two = normed_g.astype(jnp.bfloat16)
    expanded = jnp.einsum(
        "bcd,de->bce", normed_two, full_expand, preferred_element_type=jnp.float32
    )
    pre_act = expanded[..., :ffn]
    gate_part = expanded[..., ffn:]
    activated = jax.nn.gelu(pre_act, approximate=False)
    mixed = (activated * gate_part).astype(jnp.bfloat16)
    contract_acc = jnp.einsum(
        "bcd,bcf->df", upstream_half, mixed, preferred_element_type=jnp.float32
    )
    d_mixed = jnp.einsum(
        "bcd,df->bcf", upstream_half, full_contract, preferred_element_type=jnp.float32
    )
    d_expanded = jnp.concatenate(
        [d_mixed * gate_part * gelu_slope(pre_act), d_mixed * activated], axis=-1
    ).astype(jnp.bfloat16)
    expand_acc = jnp.einsum(
        "bcd,bce->de", normed_two, d_expanded, preferred_element_type=jnp.float32
    )
    ffn_sum = scatter_sum(jnp.concatenate([expand_acc, contract_acc], axis=1), axes)
    d_normed_two = jnp.einsum(
        "bce,de->bcd", d_expanded, full_expand, preferred_element_type=jnp.float32
    )
    d_resid_n, gain_two_part = norm_back(d_normed_two, norm_two, inv_two, full_gain_two)
    d_resid = upstream_half.astype(jnp.float32) + d_resid_n
    d_resid_half = d_resid.astype(jnp.bfloat16)
    d_attended = jnp.einsum(
        "bce,de->bcd", d_resid_half, full_output, preferred_element_type=jnp.float32
    )
    d_attended = d_attended.astype(jnp.bfloat16).reshape(shape_heads)
    d_probs = jnp.einsum(
        "bqhd,bkhd->bhqk", d_attended, value_rows, preferred_element_type=jnp.float32
    )
    centred = d_probs - jnp.sum(probs * d_probs, axis=-1, keepdims=True)
    d_scores = (probs * centred * scale).astype(jnp.bfloat16)
    d_key_ext = jnp.einsum(
        "bhqk,bqhd->bkhd", d_scores, q_rot, preferred_element_type=jnp.float32
    )
    d_value_ext = jnp.einsum(
        "bhqk,bqhd->bkhd", probs_half, d_attended, preferred_element_type=jnp.float32
    )
    ext_grads = jnp.stack(
        [
            d_key_ext.reshape(batch, group + 2 * half, width),
            d_value_ext.reshape(batch, group + 2 * half, width),
        ]
    )
    rims = ext_grads.astype(jnp.bfloat16)
    from_left = lax.ppermute(rims[:, :, group + half :], "seq", up).astype(jnp.float32)
    from_right = lax.ppermute(rims[:, :, :half], "seq", down).astype(jnp.float32)
    d_query = jnp.einsum(
        "bhqk,bkhd->bqhd", d_scores, key_rows, preferred_element_type=jnp.float32
    )
    output_acc = jnp.einsum(
        "bcd,bce->de", attended, d_resid_half, preferred_element_type=jnp.float32
    )
    final = resid + jnp.einsum(
        "bcf,df->bcd", mixed, full_contract, preferred_element_type=jnp.float32
    )
    own_grads = ext_grads[:, :, half : half + group]
    own_grads = own_grads + jnp.pad(
        from_left, ((0, 0), (0, 0), (0, group - half), (0, 0))
    ) + jnp.pad(from_right, ((0, 0), (0, 0), (group - half, 0), (0, 0)))
    d_key = unrotate(own_grads[0].reshape(shape_heads), cosine, sine).reshape(
        batch, group, width
    )
    d_query_flat = unrotate(d_query, cosine, sine).reshape(batch, group, width)
    d_joined = jnp.concatenate([d_query_flat, d_key, own_grads[1]], axis=-1).astype(
        jnp.bfloat16
    )
    d_normed_one = jnp.einsum(
        "bce,de->bcd", d_joined, full_joined, preferred_element_type=jnp.float32
    )
    d_source, gain_one_part = norm_back(d_normed_one, norm_one, inv_one, full_gain_one)
    input_grad = (d_resid + d_source).astype(jnp.bfloat16)
    joined_acc = jnp.einsum(
        "bcd,bce->de", normed_one, d_joined, preferred_element_type=jnp.float32
    )
    gain_parts = jnp.pad(
        jnp.stack([gain_one_part, gain_two_part], axis=1), ((0, 0), (0, LANES - 2))
    )
    last_sum = scatter_sum(jnp.concatenate([joined_acc, output_acc, gain_parts], axis=1), axes)
    return (
        final.astype(jnp.bfloat16).reshape(layer_input.shape),
        input_grad.reshape(layer_input.shape),
        last_sum[:, : 3 * width],
        last_sum[:, 3 * width : 4 * width],
        ffn_sum[:, : 2 * ffn],
        ffn_sum[:, 2 * ffn :].T,
        last_sum[:, 4 * width],
        last_sum[:, 4 * width + 1],
    )


def solution(mesh):
    placed = (
        P(None, "dp", "seq", None),
        P(None, "dp", "seq", None),
        P(("dp", "seq"), None),
        P(("dp", "seq"), None),
        P(("dp", "seq"), None),
        P(None, ("dp", "seq")),
        P(("dp", "seq")),
        P(("dp", "seq")),
    )
    return jax.shard_map(
        per_device,
        mesh=mesh,
        in_specs=placed,
        out_specs=(
            P(None, "dp", "seq", None),
            P(None, "dp", "seq", None),
            P(("dp", "seq"), None),
            P(("dp", "seq"), None),
            P(("dp", "seq"), None),
            P(None, ("dp", "seq")),
            P(("dp", "seq")),
            P(("dp", "seq")),
        ),
        check_vma=False,
    )
```

time: 778 us -> 514 us (0.66)
  waiting for transfers between devices: 476 us -> 324 us
  blocking collectives: 81.3 us -> 0 us
  matrix products: 99.6 us -> 80.6 us
  local copies, waits for them, and re-layouts: 43 us -> 26.4 us
    reduce_scatter x3 -> x0, waiting for transfers between devices: 314 us -> none  [the longest x1 125 us: per_device(): lax.psum_scatter(expand_acc, ('dp', 'seq'), scatter_dimension=0, tiled=True)]
    all_to_all x0 -> x4, waiting for transfers between devices: none -> 207 us  [scatter_sum(): lax.all_to_all(blocks, axis, 0, 0).astype(jnp.float32)]
    unnamed x2 -> x0, blocking collectives: 81.3 us -> none
    all_gather x4 -> x2, waiting for transfers between devices: 153 us -> 101 us  [the longest x1 61 us: per_device(): full_one = lax.all_gather(pack_one, axes, axis=0, tiled=True)]
    all_to_all x0 -> x4, starting transfers between devices: none -> 18.4 us  [scatter_sum(): lax.all_to_all(blocks, axis, 0, 0).astype(jnp.float32)]
    dot_general x12 -> x8, matrix products: 30.2 us -> 16.6 us  [the longest x1 4.55 us: per_device(): jnp.einsum('bcd,df->bcf', upstream_half, full_contract, preferred_element...]
    ppermute x8 -> x4, starting transfers between devices: 25.4 us -> 12.5 us  [the longest x1 5.36 us: per_device(): lax.ppermute(rims[:, :, group + half:], 'seq', up).astype(jnp.float32)]
    reduce_sum x0 -> x4, other arithmetic: none -> 11.8 us  [scatter_sum(): jnp.sum(lax.all_to_all(blocks, axis, 0, 0).astype(jnp.float32), axis=0)]
  transfers between devices with their start and end apart: 16 -> 10, of which waited for: 8 -> 8; matrix products, arithmetic and copies ran while one was open for 20% -> 13% of each run, Pallas kernels for 0% -> 0%
where the time goes in v1:
time: 514 us; the launch traced here: 513 us
  waiting for transfers between devices  324 us (63%)
  matrix products  80.6 us (16%)
  other arithmetic  36.5 us (7%)
  starting transfers between devices  31 us (6%)
  local copies, waits for them, and re-layouts  26.4 us (5%)
  between operations  14.8 us (3%)
    all_to_all x4, waiting for transfers between devices, scatter_sum(): lax.all_to_all(blocks, axis, 0, 0).astype(jnp.float32)  207 us
    all_gather x1, waiting for transfers between devices, per_device(): full_one = lax.all_gather(pack_one, axes, axis=0, tiled=True)  61 us
    all_gather x1, waiting for transfers between devices, per_device(): full_two = lax.all_gather(pack_two, axes, axis=0, tiled=True)  40.2 us
    dot_general x1, matrix products, per_device(): jnp.einsum('bhqk,bqhd->bkhd', d_scores, q_rot, preferred_element_type=jnp...  21.4 us
    dot_general x1, matrix products, per_device(): jnp.einsum('bhqk,bkhd->bqhd', d_scores, key_rows, preferred_element_type=...  21.2 us
    all_to_all x4, starting transfers between devices, scatter_sum(): lax.all_to_all(blocks, axis, 0, 0).astype(jnp.float32)  18.4 us
    reduce_sum x4, other arithmetic, scatter_sum(): jnp.sum(lax.all_to_all(blocks, axis, 0, 0).astype(jnp.float32), axis=0)  11.8 us
  transfers between devices with their start and end apart: 10, of which 8 were waited for; matrix products, arithmetic and copies ran while one was open for 13% of the time, Pallas kernels for 0%

profile of v1, /device:TPU:0, one launch (start us, length us, event | category | flops | bytes accessed | tf_op | source)
XLA Modules:
  0.0 513.3 jit_solution(2733188091576506096)
XLA Ops:
  8.0 1.6 fusion.76
  9.6 1.6 pad_maximum_fusion.17
  13.9 61.0 %all-gather.3.cloned.1.call-done = bf16[768,2432]{1,0:T(8,128)(2,1)} async-done(((bf16[24,2432]{1,0:T(8,128)(2,1)}), bf16[768,2432]{1,0:T(8,128)(2,1)}) %all-gather.3.cloned.1.call-update) | async-done | bytes 3735568 | tf_op jit(solution)/shard_map/all_gather | solution.py:102
  74.9 1.3 convert_reduce_fusion.3
  76.2 3.3 fusion.5
  79.6 1.4 copy-done.13
  83.3 1.3 collective-permute-start.1
  84.6 4.6 collective-permute-start
  89.9 8.0 %collective-permute-done.1 = bf16[2,2,64,768]{3,2,1,0:T(8,128)(2,1)S(1)} collective-permute-done((bf16[2,2,64,768]{3,2,1,0:T(8,128)(2,1)S(1)}, bf16[2,2,64,768]{3,2,1,0:T(8,128)(2,1)S(1)}, u32[]{:S(2)}, u32[]{:S(2)}) %collective-permute-start.1) | collective-permute-done | bytes 393248 | tf_op jit(solution)/shard_map/ppermute | solution.py:125
  97.9 7.7 %collective-permute-done = bf16[2,2,64,768]{3,2,1,0:T(8,128)(2,1)S(1)} collective-permute-done((bf16[2,2,64,768]{3,2,1,0:T(8,128)(2,1)S(1)}, bf16[2,2,64,768]{3,2,1,0:T(8,128)(2,1)S(1)}, u32[]{:S(2)}, u32[]{:S(2)}) %collective-permute-start) | collective-permute-done | bytes 393248 | tf_op jit(solution)/shard_map/ppermute | solution.py:124
  108.1 1.9 fusion.10
  111.9 1.7 convolution_convert_fusion.1
  113.6 40.2 %all-gather.5.cloned.1.call-done = bf16[768,4224]{1,0:T(8,128)(2,1)} async-done(((bf16[24,4224]{1,0:T(8,128)(2,1)}), bf16[768,4224]{1,0:T(8,128)(2,1)}) %all-gather.5.cloned.1.call-update) | async-done | bytes 6488080 | tf_op jit(solution)/shard_map/all_gather | solution.py:103
  153.8 2.0 fusion.107
  156.0 3.5 fusion.7
  160.0 4.5 multiply_convert_fusion.1
  164.5 1.8 multiply_reduce_fusion.1
  168.8 1.9 copy.100
  170.7 3.6 fusion.108
  174.3 2.1 fusion.77
  176.5 21.4 %fusion.12 = f32[2,12,64,256]{3,2,1,0:T(8,128)} fusion(f32[2,12,128,256]{3,2,1,0:T(8,128)} %fusion.108, f32[2,12,128,256]{3,2,1,0:T(8,128)S(1)} %get-tuple-element.77, f32[2,12,128]{2,1,0:T(8,128)} %copy-done.33, pred[128,256]{1,0:T(8,128)(4,1)} %fusion.75, bf16[2,128,12,32]{1,3,2,0:T(8,128)(2,1)} %copy-done.19, bf16[2,128,12,32]{1,3,2,0:T(8,128)(2,1)} %copy-done.18), kind=kOutput, calls=%fused_computation.28 | convolution fusion | flops 110103808 | bytes 8302592 | tf_op jit(solution)/shard_map/bhqk,bqhd->bkhd/dot_general | solution.py:184
  197.9 3.0 copy.101
  200.9 3.1 copy.102
  204.0 2.1 fusion.2
  208.4 5.4 %collective-permute-start.2 = (bf16[2,2,64,768]{3,2,1,0:T(8,128)(2,1)}, bf16[2,2,64,768]{3,2,1,0:T(8,128)(2,1)}, u32[]{:S(2)}, u32[]{:S(2)}) collective-permute-start(bf16[2,2,64,768]{3,2,1,0:T(8,128)(2,1)} %get-tuple-element.55), channel_id=1, source_target_pairs={{0,1},{1,2},{2,3},{3,4},{4,5},{5,6},{6,7},{8,9},{9,10},{10,11},{11... | collective-permute-start | bytes 1179656 | tf_op jit(solution)/shard_map/ppermute | solution.py:197
  213.8 21.2 %fusion.23 = f32[2,128,12,64]{1,3,2,0:T(8,128)} fusion(bf16[2,256,12,64]{1,3,2,0:T(8,128)(2,1)} %bitcast.181, f32[2,12,128,256]{3,2,1,0:T(8,128)} %fusion.108, f32[2,12,128,256]{3,2,1,0:T(8,128)S(1)} %get-tuple-element.77, f32[2,12,128]{2,1,0:T(8,128)} %copy-done.33, pred[128,256]{1,0:T(8,128)(4,1)} %fusion.75), kind=kOutput, calls=%fused_computation.40 | convolution fusion | flops 109317376 | bytes 7909376 | tf_op jit(solution)/shard_map/bhqk,bkhd->bqhd/dot_general | solution.py:199
  235.0 1.4 stack.37
  236.4 1.7 bitcast_convert_fusion.2
  238.1 1.5 fusion.19
  240.8 1.3 add_convert_fusion.1
  243.9 3.1 fusion.4
  248.5 2.2 bitcast_convert_fusion.1
  250.8 2.4 pad_maximum_fusion.1
  253.2 5.4 %all-to-all-start = ((bf16[4,192,3200]{2,1,0:T(8,128)(2,1)}), bf16[4,192,3200]{2,1,0:T(8,128)(2,1)}, u32[]{:S(2)}, u32[]{:S(2)}) async-start(bf16[4,192,3200]{2,1,0:T(8,128)(2,1)} %pad_maximum_fusion.1), calls=%async_computation | async-start | bytes 9830400 | tf_op jit(solution)/shard_map/all_to_all | solution.py:26
  258.7 1.5 multiply_convert_fusion.2
  262.3 2.8 pad_maximum_fusion
  265.1 49.2 %all-to-all-done = bf16[4,192,3200]{2,1,0:T(8,128)(2,1)} async-done(((bf16[4,192,3200]{2,1,0:T(8,128)(2,1)}), bf16[4,192,3200]{2,1,0:T(8,128)(2,1)}, u32[]{:S(2)}, u32[]{:S(2)}) %all-to-all-start) | async-done | bytes 4915232 | tf_op jit(solution)/shard_map/all_to_all | solution.py:26
  314.3 5.1 all-to-all-start.2
  319.4 4.7 convert_reduce_fusion.1
  324.1 55.4 %all-to-all-done.2 = bf16[4,192,3456]{2,1,0:T(8,128)(2,1)} async-done(((bf16[4,192,3456]{2,1,0:T(8,128)(2,1)}), bf16[4,192,3456]{2,1,0:T(8,128)(2,1)}, u32[]{:S(2)}, u32[]{:S(2)}) %all-to-all-start.2) | async-done | bytes 5308448 | tf_op jit(solution)/shard_map/all_to_all | solution.py:26
  379.5 4.3 all-to-all-start.1
  383.8 5.1 convert_reduce_fusion
  388.9 50.6 %all-to-all-done.1 = f32[8,24,3200]{2,1,0:T(8,128)S(1)} async-done(((f32[8,24,3200]{2,1,0:T(8,128)}), f32[8,24,3200]{2,1,0:T(8,128)S(1)}, u32[]{:S(2)}, u32[]{:S(2)}) %all-to-all-start.1) | async-done | bytes 2457632 | tf_op jit(solution)/shard_map/all_to_all | solution.py:26
  439.5 1.6 copy-done.7
  441.0 3.6 all-to-all-start.3
  444.7 3.2 fusion.28
  449.1 1.8 reduce_sum.157
  453.0 52.0 %all-to-all-done.3 = f32[8,24,3456]{2,1,0:T(8,128)S(1)} async-done(((f32[8,24,3456]{2,1,0:T(8,128)}), f32[8,24,3456]{2,1,0:T(8,128)S(1)}, u32[]{:S(2)}, u32[]{:S(2)}) %all-to-all-start.3) | async-done | bytes 2654240 | tf_op jit(solution)/shard_map/all_to_all | solution.py:26
  (149 shorter events, 27.3 us)
Async XLA Ops:
  7.2 67.7 %all-gather.3.cloned.1.call-start = ((), (), s32[]{:S(2)}) async-start(), calls=%async_computation.4 | async-start | bytes 3852288 | tf_op jit(solution)/shard_map/all_gather | solution.py:102
  9.6 144.2 %all-gather.5.cloned.1.call-start = ((), (), s32[]{:S(2)}) async-start(), calls=%async_computation.5 | async-start | bytes 6690816 | tf_op jit(solution)/shard_map/all_gather | solution.py:103
  13.7 65.8 %copy-start.38 = (f32[2,128]{1,0:T(2,128)}, f32[2,128]{1,0:T(2,128)S(1)}, u32[]{:S(2)}) copy-start(f32[2,128]{1,0:T(2,128)S(1)} %add_rsqrt_fusion.1) | copy-start | bytes 3076
  13.9 67.7 %copy-start.31 = (f32[128,32]{0,1:T(8,128)}, f32[128,32]{0,1:T(8,128)S(1)}, u32[]{:S(2)}) copy-start(f32[128,32]{0,1:T(8,128)S(1)} %get-tuple-element.74) | copy-start | bytes 49156
  13.9 67.7 %copy-start.32 = (f32[128,32]{0,1:T(8,128)}, f32[128,32]{0,1:T(8,128)S(1)}, u32[]{:S(2)}) copy-start(f32[128,32]{0,1:T(8,128)S(1)} %get-tuple-element.75) | copy-start | bytes 49156
  79.5 1.5 copy-start.13
  81.8 26.3 %copy-start.18 = (bf16[2,128,12,32]{1,3,2,0:T(8,128)(2,1)}, bf16[2,128,12,32]{1,3,2,0:T(8,128)(2,1)S(1)}, u32[]{:S(2)}) copy-start(bf16[2,128,12,32]{1,3,2,0:T(8,128)(2,1)S(1)} %get-tuple-element.63) | copy-start | bytes 589828
  81.8 26.3 %copy-start.19 = (bf16[2,128,12,32]{1,3,2,0:T(8,128)(2,1)}, bf16[2,128,12,32]{1,3,2,0:T(8,128)(2,1)S(1)}, u32[]{:S(2)}) copy-start(bf16[2,128,12,32]{1,3,2,0:T(8,128)(2,1)S(1)} %get-tuple-element.64) | copy-start | bytes 589828
  83.3 14.6 %collective-permute-start.1 = (bf16[2,2,64,768]{3,2,1,0:T(8,128)(2,1)S(1)}, bf16[2,2,64,768]{3,2,1,0:T(8,128)(2,1)S(1)}, u32[]{:S(2)}, u32[]{:S(2)}) collective-permute-start(bf16[2,2,64,768]{3,2,1,0:T(8,128)(2,1)S(1)} %get-tuple-element.68), channel_id=1, source_target_pairs={{1,0},{2,1},{3,2},{4,3},{5,4},{6,5},{7,6},{9,8},{10,9},{11,10},{12... | collective-permute-start | bytes 1179656 | tf_op jit(solution)/shard_map/ppermute | solution.py:125
  84.6 21.0 %collective-permute-start = (bf16[2,2,64,768]{3,2,1,0:T(8,128)(2,1)S(1)}, bf16[2,2,64,768]{3,2,1,0:T(8,128)(2,1)S(1)}, u32[]{:S(2)}, u32[]{:S(2)}) collective-permute-start(bf16[2,2,64,768]{3,2,1,0:T(8,128)(2,1)S(1)} %get-tuple-element.67), channel_id=1, source_target_pairs={{0,1},{1,2},{2,3},{3,4},{4,5},{5,6},{6,7},{8,9},{9,10},{10,11},{11... | collective-permute-start | bytes 1179656 | tf_op jit(solution)/shard_map/ppermute | solution.py:124
  108.1 1.9 copy-start.25
  110.0 1.9 copy-start.11
  111.9 41.9 %copy-start.5 = (bf16[2,1,128,768]{3,2,1,0:T(8,128)(2,1)S(1)}, bf16[2,1,128,768]{3,2,1,0:T(8,128)(2,1)}, u32[]{:S(2)}) copy-start(bf16[2,1,128,768]{3,2,1,0:T(8,128)(2,1)} %param.8) | copy-start | bytes 1179652
  155.7 10.6 %copy-start = (f32[2,128,768]{2,1,0:T(8,128)}, f32[2,128,768]{2,1,0:T(8,128)S(1)}, u32[]{:S(2)}) copy-start(f32[2,128,768]{2,1,0:T(8,128)S(1)} %get-tuple-element.79) | copy-start | bytes 2359300
  155.8 4.2 copy-start.17
  156.0 10.3 %copy-start.35 = (f32[2,128]{1,0:T(2,128)}, f32[2,128]{1,0:T(2,128)S(1)}, u32[]{:S(2)}) copy-start(f32[2,128]{1,0:T(2,128)S(1)} %add_rsqrt_fusion) | copy-start | bytes 3076
  156.0 4.0 copy-start.14
  160.0 4.6 copy-start.24
  164.5 1.8 copy-start.20
  164.5 1.8 copy-start.22
  170.7 3.6 copy-start.8
  170.7 3.6 copy-start.26
  170.7 3.6 copy-start.34
  207.1 31.0 %collective-permute-start.3 = (bf16[2,2,64,768]{3,2,1,0:T(8,128)(2,1)}, bf16[2,2,64,768]{3,2,1,0:T(8,128)(2,1)}, u32[]{:S(2)}, u32[]{:S(2)}) collective-permute-start(bf16[2,2,64,768]{3,2,1,0:T(8,128)(2,1)} %get-tuple-element.56), channel_id=1, source_target_pairs={{1,0},{2,1},{3,2},{4,3},{5,4},{6,5},{7,6},{9,8},{10,9},{11,10},{12... | collective-permute-start | bytes 1179656 | tf_op jit(solution)/shard_map/ppermute | solution.py:198
  208.4 29.7 %collective-permute-start.2 = (bf16[2,2,64,768]{3,2,1,0:T(8,128)(2,1)}, bf16[2,2,64,768]{3,2,1,0:T(8,128)(2,1)}, u32[]{:S(2)}, u32[]{:S(2)}) collective-permute-start(bf16[2,2,64,768]{3,2,1,0:T(8,128)(2,1)} %get-tuple-element.55), channel_id=1, source_target_pairs={{0,1},{1,2},{2,3},{3,4},{4,5},{5,6},{6,7},{8,9},{9,10},{10,11},{11... | collective-permute-start | bytes 1179656 | tf_op jit(solution)/shard_map/ppermute | solution.py:197
  235.0 3.1 copy-start.2
  242.1 1.7 copy-start.27
  243.9 3.1 copy-start.39
  243.9 4.2 copy-start.37
  247.0 3.7 copy-start.9
  253.2 5.4 %copy-start.16 = (f32[2,128,1152]{2,1,0:T(8,128)S(1)}, f32[2,128,1152]{2,1,0:T(8,128)}, u32[]{:S(2)}) copy-start(f32[2,128,1152]{2,1,0:T(8,128)} %get-tuple-element.51) | copy-start | bytes 3538948
  253.2 61.1 %all-to-all-start = ((bf16[4,192,3200]{2,1,0:T(8,128)(2,1)}), bf16[4,192,3200]{2,1,0:T(8,128)(2,1)}, u32[]{:S(2)}, u32[]{:S(2)}) async-start(bf16[4,192,3200]{2,1,0:T(8,128)(2,1)} %pad_maximum_fusion.1), calls=%async_computation | async-start | bytes 9830400 | tf_op jit(solution)/shard_map/all_to_all | solution.py:26
  258.6 1.6 copy-start.15
  258.6 2.3 copy-start.1
  258.6 2.3 copy-start.21
  258.7 2.3 copy-start.23
  258.7 2.3 copy-start.36
  260.2 2.0 copy-start.12
  314.3 65.2 %all-to-all-start.2 = ((bf16[4,192,3456]{2,1,0:T(8,128)(2,1)}), bf16[4,192,3456]{2,1,0:T(8,128)(2,1)}, u32[]{:S(2)}, u32[]{:S(2)}) async-start(bf16[4,192,3456]{2,1,0:T(8,128)(2,1)} %pad_maximum_fusion), calls=%async_computation.2 | async-start | bytes 10616832 | tf_op jit(solution)/shard_map/all_to_all | solution.py:26
  379.5 60.0 %all-to-all-start.1 = ((f32[8,24,3200]{2,1,0:T(8,128)}), f32[8,24,3200]{2,1,0:T(8,128)S(1)}, u32[]{:S(2)}, u32[]{:S(2)}) async-start(f32[8,24,3200]{2,1,0:T(8,128)} %bitcast.46), calls=%async_computation.1 | async-start | bytes 4915200 | tf_op jit(solution)/shard_map/all_to_all | solution.py:26
  439.4 1.6 copy-start.7
  441.0 64.0 %all-to-all-start.3 = ((f32[8,24,3456]{2,1,0:T(8,128)}), f32[8,24,3456]{2,1,0:T(8,128)S(1)}, u32[]{:S(2)}, u32[]{:S(2)}) async-start(f32[8,24,3456]{2,1,0:T(8,128)} %bitcast.172), calls=%async_computation.3 | async-start | bytes 5308416 | tf_op jit(solution)/shard_map/all_to_all | solution.py:26
  444.6 3.3 copy-start.42
  444.6 3.3 copy-start.41
  444.7 3.3 copy-start.4
  444.7 3.3 copy-start.6
  444.7 3.3 copy-start.10
  444.7 3.3 copy-start.40
  (5 other events, 4.5 us)
Sparse Core Ops, SparseCore 0:
  11.4 63.4 all-gather.2
  78.3 75.4 all-gather.4

commit v2 on v1

--- a/solution.py
+++ b/solution.py
@@ -19,12 +19,31 @@
 
 
 def scatter_sum(value, axes):
-    value = value.astype(jnp.bfloat16)
-    for axis in axes:
-        size = lax.axis_size(axis)
-        blocks = value.reshape(size, value.shape[0] // size, value.shape[1])
-        value = jnp.sum(lax.all_to_all(blocks, axis, 0, 0).astype(jnp.float32), axis=0)
-    return value
+    outer, inner = axes
+    outer_size, inner_size = (lax.axis_size(outer), lax.axis_size(inner))
+    pairs = outer_size // 2
+    place = lax.axis_index(outer)
+    core = place % 2
+    blocks = value.reshape(pairs, 2, value.shape[0] // outer_size, value.shape[1])
+    other = lax.dynamic_index_in_dim(blocks, 1 - core, axis=1, keepdims=False)
+    own = lax.dynamic_index_in_dim(blocks, core, axis=1, keepdims=False)
+    swap = [(i, i ^ 1) for i in range(outer_size)]
+    value = own + lax.ppermute(other, outer, swap)
+    if pairs == 2:
+        line = place // 2
+        other = lax.dynamic_index_in_dim(value, 1 - line, axis=0, keepdims=False)
+        own = lax.dynamic_index_in_dim(value, line, axis=0, keepdims=False)
+        swap = [(i, i ^ 2) for i in range(outer_size)]
+        arrived = lax.ppermute(other.astype(jnp.bfloat16), outer, swap)
+        value = own + arrived.astype(jnp.float32)
+    else:
+        groups = [list(range(c, outer_size, 2)) for c in range(2)]
+        arrived = lax.all_to_all(
+            value.astype(jnp.bfloat16), outer, 0, 0, axis_index_groups=groups
+        )
+        value = jnp.sum(arrived.astype(jnp.float32), axis=0)
+    blocks = value.reshape(inner_size, value.shape[0] // inner_size, value.shape[1])
+    return jnp.sum(lax.all_to_all(blocks, inner, 0, 0), axis=0)
 
 
 def norm_apply(values, gain):
@@ -165,7 +184,10 @@
     expand_acc = jnp.einsum(
         "bcd,bce->de", normed_two, d_expanded, preferred_element_type=jnp.float32
     )
-    ffn_sum = scatter_sum(jnp.concatenate([expand_acc, contract_acc], axis=1), axes)
+    ffn_grads, d_expanded = lax.optimization_barrier(
+        (jnp.concatenate([expand_acc, contract_acc], axis=1), d_expanded)
+    )
+    ffn_sum = scatter_sum(ffn_grads, axes)
     d_normed_two = jnp.einsum(
         "bce,de->bcd", d_expanded, full_expand, preferred_element_type=jnp.float32
     )

time: 514 us -> 465 us (0.905)
  waiting for transfers between devices: 324 us -> 250 us
  matrix products: 80.6 us -> 92.4 us
  other arithmetic: 36.5 us -> 46.8 us
  local copies, waits for them, and re-layouts: 26.4 us -> 36.2 us
  starting transfers between devices: 31 us -> 23.8 us
    all_to_all x4 -> x2, waiting for transfers between devices: 207 us -> 70.8 us  [scatter_sum(): return jnp.sum(lax.all_to_all(blocks, inner, 0, 0), axis=0)]
    ppermute x0 -> x4, waiting for transfers between devices: none -> 61.7 us  [the longest x2 56.4 us: scatter_sum(): arrived = lax.ppermute(other.astype(jnp.bfloat16), outer, swap)]
    add x0 -> x4, other arithmetic: none -> 14.1 us  [the longest x2 9 us: scatter_sum(): value = own + lax.ppermute(other, outer, swap)]
    reduce_sum x5 -> x2, other arithmetic: 12.9 us -> 1.99 us  [scatter_sum(): return jnp.sum(lax.all_to_all(blocks, inner, 0, 0), axis=0)]
    all_to_all x4 -> x2, starting transfers between devices: 18.4 us -> 7.88 us  [scatter_sum(): return jnp.sum(lax.all_to_all(blocks, inner, 0, 0), axis=0)]
    unnamed x87 -> x84, local copies, waits for them, and re-layouts: 6.4 us -> 12.5 us
    concatenate x1, other arithmetic: 2.8 us -> 8.82 us  [per_device(): jnp.concatenate([expand_acc, contract_acc], axis=1)]
    squeeze x0 -> x2, local copies, waits for them, and re-layouts: none -> 5.43 us  [scatter_sum(): other = lax.dynamic_index_in_dim(blocks, 1 - core, axis=1, keepdims=False)]
  transfers between devices with their start and end apart: 10 -> 12, of which waited for: 8 -> 9; matrix products, arithmetic and copies ran while one was open for 13% -> 15% of each run, Pallas kernels for 0% -> 0%
where the time goes in v2:
time: 465 us; the launch traced here: 464 us
  waiting for transfers between devices  250 us (54%)
  matrix products  92.4 us (20%)
  other arithmetic  46.8 us (10%)
  local copies, waits for them, and re-layouts  36.2 us (8%)
  starting transfers between devices  23.8 us (5%)
  between operations  14.8 us (3%)
    all_to_all x2, waiting for transfers between devices, scatter_sum(): return jnp.sum(lax.all_to_all(blocks, inner, 0, 0), axis=0)  70.8 us
    all_gather x1, waiting for transfers between devices, per_device(): full_one = lax.all_gather(pack_one, axes, axis=0, tiled=True)  61 us
    ppermute x2, waiting for transfers between devices, scatter_sum(): arrived = lax.ppermute(other.astype(jnp.bfloat16), outer, swap)  56.4 us
    all_gather x1, waiting for transfers between devices, per_device(): full_two = lax.all_gather(pack_two, axes, axis=0, tiled=True)  40.4 us
    dot_general x1, matrix products, per_device(): jnp.einsum('bhqk,bqhd->bkhd', d_scores, q_rot, preferred_element_type=jnp...  21.5 us
    dot_general x1, matrix products, per_device(): jnp.einsum('bhqk,bkhd->bqhd', d_scores, key_rows, preferred_element_type=...  21.3 us
    unnamed x84, local copies, waits for them, and re-layouts  12.5 us
  transfers between devices with their start and end apart: 12, of which 9 were waited for; matrix products, arithmetic and copies ran while one was open for 15% of the time, Pallas kernels for 0%

profile of v2, /device:TPU:0, one launch (start us, length us, event | category | flops | bytes accessed | tf_op | source)
XLA Modules:
  0.0 463.5 jit_solution(6078588214111812776)
XLA Ops:
  9.6 1.6 pad_maximum_fusion.14
  13.9 61.0 %all-gather.3.cloned.1.call-done = bf16[768,2432]{1,0:T(8,128)(2,1)} async-done(((bf16[24,2432]{1,0:T(8,128)(2,1)}), bf16[768,2432]{1,0:T(8,128)(2,1)}) %all-gather.3.cloned.1.call-update) | async-done | bytes 3735568 | tf_op jit(solution)/shard_map/all_gather | solution.py:121
  76.2 3.3 fusion.4
  84.5 4.6 collective-permute-start
  89.8 7.9 %collective-permute-done.1 = bf16[2,2,64,768]{3,2,1,0:T(8,128)(2,1)S(1)} collective-permute-done((bf16[2,2,64,768]{3,2,1,0:T(8,128)(2,1)S(1)}, bf16[2,2,64,768]{3,2,1,0:T(8,128)(2,1)S(1)}, u32[]{:S(2)}, u32[]{:S(2)}) %collective-permute-start.1) | collective-permute-done | bytes 393248 | tf_op jit(solution)/shard_map/ppermute | solution.py:144
  97.8 7.7 %collective-permute-done = bf16[2,2,64,768]{3,2,1,0:T(8,128)(2,1)S(1)} collective-permute-done((bf16[2,2,64,768]{3,2,1,0:T(8,128)(2,1)S(1)}, bf16[2,2,64,768]{3,2,1,0:T(8,128)(2,1)S(1)}, u32[]{:S(2)}, u32[]{:S(2)}) %collective-permute-start) | collective-permute-done | bytes 393248 | tf_op jit(solution)/shard_map/ppermute | solution.py:143
  108.0 1.9 fusion.9
  111.9 1.7 convolution_convert_fusion.1
  113.6 40.4 %all-gather.5.cloned.1.call-done = bf16[768,4224]{1,0:T(8,128)(2,1)} async-done(((bf16[24,4224]{1,0:T(8,128)(2,1)}), bf16[768,4224]{1,0:T(8,128)(2,1)}) %all-gather.5.cloned.1.call-update) | async-done | bytes 6488080 | tf_op jit(solution)/shard_map/all_gather | solution.py:122
  154.0 2.0 fusion.104
  156.3 3.2 fusion.6
  159.5 5.0 %multiply_convert_fusion.1 = (bf16[2,128,1152]{2,1,0:T(8,128)(2,1)S(1)}, f32[2,128,1152]{2,1,0:T(8,128)S(1)}, bf16[2,128,1152]{2,1,0:T(8,128)(2,1)S(1)}) fusion(f32[2,128,2304]{2,1,0:T(8,128)S(1)} %fusion.6, bf16[2,1,128,768]{3,2,1,0:T(8,128)(2,1)S(1)} %copy-done.18, bf16[768,4224]{1,0:T(8,128)(2,1)} %all-gather.5.cloned.1.call-done), kind=kOutput, calls=%fused_computation.66 | convolution fusion | flops 475693056 | bytes 6881280 | tf_op jit(solution)/shard_map/bcd,df->bcf/dot_general | solution.py:178
  164.6 4.2 convolution_bitcast_fusion.1
  170.8 2.5 convolution_bitcast_fusion.2
  173.2 8.8 %pad_maximum_fusion = f32[768,3456]{1,0:T(8,128)} fusion(f32[768,1152]{1,0:T(8,128)} %convolution_bitcast_fusion.2, f32[768,2304]{1,0:T(8,128)} %convolution_bitcast_fusion.1), kind=kLoop, calls=%fused_computation.1 | loop fusion | flops 2654208 | bytes 21233664 | tf_op jit(solution)/shard_map/concatenate | solution.py:188
  182.1 4.5 multiply_reduce_fusion.1
  187.9 2.5 convolution_convert_fusion
  190.4 1.9 copy.88
  192.3 3.7 fusion.105
  196.0 2.1 fusion.76
  198.1 21.5 %fusion.11 = f32[2,12,64,256]{3,2,1,0:T(8,128)} fusion(f32[2,12,128,256]{3,2,1,0:T(8,128)} %fusion.105, f32[2,12,128,256]{3,2,1,0:T(8,128)S(1)} %get-tuple-element.72, f32[2,12,128]{2,1,0:T(8,128)} %copy-done.29, pred[128,256]{1,0:T(8,128)(4,1)} %fusion.74, bf16[2,128,12,32]{1,3,2,0:T(8,128)(2,1)} %copy-done.21, bf16[2,128,12,32]{1,3,2,0:T(8,128)(2,1)} %copy-done.20), kind=kOutput, calls=%fused_computation.33 | convolution fusion | flops 110103808 | bytes 8302592 | tf_op jit(solution)/shard_map/bhqk,bqhd->bkhd/dot_general | solution.py:206
  219.6 3.0 copy.89
  222.6 3.2 copy.90
  225.8 2.2 fusion.1
  230.3 5.3 %collective-permute-start.2 = (bf16[2,2,64,768]{3,2,1,0:T(8,128)(2,1)}, bf16[2,2,64,768]{3,2,1,0:T(8,128)(2,1)}, u32[]{:S(2)}, u32[]{:S(2)}) collective-permute-start(bf16[2,2,64,768]{3,2,1,0:T(8,128)(2,1)} %get-tuple-element.51), channel_id=1, source_target_pairs={{0,1},{1,2},{2,3},{3,4},{4,5},{5,6},{6,7},{8,9},{9,10},{10,11},{11... | collective-permute-start | bytes 1179656 | tf_op jit(solution)/shard_map/ppermute | solution.py:219
  235.7 1.9 convolution_bitcast_fusion.4
  237.6 21.3 %fusion.23 = f32[2,128,12,64]{1,3,2,0:T(8,128)} fusion(bf16[2,256,12,64]{1,3,2,0:T(8,128)(2,1)} %bitcast.181, f32[2,12,128,256]{3,2,1,0:T(8,128)} %fusion.105, f32[2,12,128,256]{3,2,1,0:T(8,128)S(1)} %get-tuple-element.72, f32[2,12,128]{2,1,0:T(8,128)} %copy-done.29, pred[128,256]{1,0:T(8,128)(4,1)} %fusion.74), kind=kOutput, calls=%fused_computation.47 | convolution fusion | flops 109317376 | bytes 7909376 | tf_op jit(solution)/shard_map/bhqk,bkhd->bqhd/dot_general | solution.py:221
  258.9 1.7 fusion.18
  263.9 4.1 convolution_bitcast_fusion
  268.1 3.8 fusion.59
  272.1 3.6 select_maximum_fusion
  275.7 2.7 dynamic-slice_bitcast_fusion.1
  278.4 4.0 copy-done
  282.3 2.8 dynamic-slice_bitcast_fusion
  285.6 5.2 %collective-permute-done.4 = f32[2,192,3200]{2,1,0:T(8,128)} collective-permute-done((f32[2,192,3200]{2,1,0:T(8,128)}, f32[2,192,3200]{2,1,0:T(8,128)}, u32[]{:S(2)}, u32[]{:S(2)}) %collective-permute-start.4) | collective-permute-done | bytes 4915232 | tf_op jit(solution)/shard_map/ppermute | solution.py:31
  290.8 4.4 bitcast_add_fusion.1
  295.2 2.3 copy-done.1
  299.1 27.6 %collective-permute-done.5 = bf16[192,3200]{1,0:T(8,128)(2,1)S(1)} collective-permute-done((bf16[192,3200]{1,0:T(8,128)(2,1)S(1)}, bf16[192,3200]{1,0:T(8,128)(2,1)S(1)}, u32[]{:S(2)}, u32[]{:S(2)}) %collective-permute-start.5) | collective-permute-done | bytes 1228832 | tf_op jit(solution)/shard_map/ppermute | solution.py:37
  326.7 3.3 bitcast_add_fusion.3
  330.1 4.1 all-to-all-start
  334.2 4.6 bitcast_add_fusion
  340.3 28.8 %collective-permute-done.7 = bf16[192,3456]{1,0:T(8,128)(2,1)S(1)} collective-permute-done((bf16[192,3456]{1,0:T(8,128)(2,1)S(1)}, bf16[192,3456]{1,0:T(8,128)(2,1)S(1)}, u32[]{:S(2)}, u32[]{:S(2)}) %collective-permute-start.7) | collective-permute-done | bytes 1327136 | tf_op jit(solution)/shard_map/ppermute | solution.py:37
  369.1 1.7 bitcast_add_fusion.2
  370.9 18.7 %all-to-all-done = f32[8,24,3200]{2,1,0:T(8,128)S(1)} async-done(((f32[8,24,3200]{2,1,0:T(8,128)}), f32[8,24,3200]{2,1,0:T(8,128)S(1)}, u32[]{:S(2)}, u32[]{:S(2)}) %all-to-all-start) | async-done | bytes 2457632 | tf_op jit(solution)/shard_map/all_to_all | solution.py:46
  391.0 3.8 all-to-all-start.1
  394.9 3.3 fusion.29
  399.3 1.8 reduce_sum.138
  403.1 52.0 %all-to-all-done.1 = f32[8,24,3456]{2,1,0:T(8,128)S(1)} async-done(((f32[8,24,3456]{2,1,0:T(8,128)}), f32[8,24,3456]{2,1,0:T(8,128)S(1)}, u32[]{:S(2)}, u32[]{:S(2)}) %all-to-all-start.1) | async-done | bytes 2654240 | tf_op jit(solution)/shard_map/all_to_all | solution.py:46
  (156 shorter events, 35.4 us)
Async XLA Ops:
  7.2 67.7 %all-gather.3.cloned.1.call-start = ((), (), s32[]{:S(2)}) async-start(), calls=%async_computation.2 | async-start | bytes 3852288 | tf_op jit(solution)/shard_map/all_gather | solution.py:121
  9.6 144.4 %all-gather.5.cloned.1.call-start = ((), (), s32[]{:S(2)}) async-start(), calls=%async_computation.3 | async-start | bytes 6690816 | tf_op jit(solution)/shard_map/all_gather | solution.py:122
  13.9 67.6 %copy-start.25 = (f32[128,32]{0,1:T(8,128)}, f32[128,32]{0,1:T(8,128)S(1)}, u32[]{:S(2)}) copy-start(f32[128,32]{0,1:T(8,128)S(1)} %get-tuple-element.69) | copy-start | bytes 49156
  13.9 67.6 %copy-start.27 = (f32[128,32]{0,1:T(8,128)}, f32[128,32]{0,1:T(8,128)S(1)}, u32[]{:S(2)}) copy-start(f32[128,32]{0,1:T(8,128)S(1)} %get-tuple-element.70) | copy-start | bytes 49156
  79.5 1.4 copy-start.15
  81.7 26.4 %copy-start.20 = (bf16[2,128,12,32]{1,3,2,0:T(8,128)(2,1)}, bf16[2,128,12,32]{1,3,2,0:T(8,128)(2,1)S(1)}, u32[]{:S(2)}) copy-start(bf16[2,128,12,32]{1,3,2,0:T(8,128)(2,1)S(1)} %get-tuple-element.59) | copy-start | bytes 589828
  81.7 26.4 %copy-start.21 = (bf16[2,128,12,32]{1,3,2,0:T(8,128)(2,1)}, bf16[2,128,12,32]{1,3,2,0:T(8,128)(2,1)S(1)}, u32[]{:S(2)}) copy-start(bf16[2,128,12,32]{1,3,2,0:T(8,128)(2,1)S(1)} %get-tuple-element.60) | copy-start | bytes 589828
  83.2 14.6 %collective-permute-start.1 = (bf16[2,2,64,768]{3,2,1,0:T(8,128)(2,1)S(1)}, bf16[2,2,64,768]{3,2,1,0:T(8,128)(2,1)S(1)}, u32[]{:S(2)}, u32[]{:S(2)}) collective-permute-start(bf16[2,2,64,768]{3,2,1,0:T(8,128)(2,1)S(1)} %get-tuple-element.64), channel_id=1, source_target_pairs={{1,0},{2,1},{3,2},{4,3},{5,4},{6,5},{7,6},{9,8},{10,9},{11,10},{12... | collective-permute-start | bytes 1179656 | tf_op jit(solution)/shard_map/ppermute | solution.py:144
  84.5 21.0 %collective-permute-start = (bf16[2,2,64,768]{3,2,1,0:T(8,128)(2,1)S(1)}, bf16[2,2,64,768]{3,2,1,0:T(8,128)(2,1)S(1)}, u32[]{:S(2)}, u32[]{:S(2)}) collective-permute-start(bf16[2,2,64,768]{3,2,1,0:T(8,128)(2,1)S(1)} %get-tuple-element.63), channel_id=1, source_target_pairs={{0,1},{1,2},{2,3},{3,4},{4,5},{5,6},{6,7},{8,9},{9,10},{10,11},{11... | collective-permute-start | bytes 1179656 | tf_op jit(solution)/shard_map/ppermute | solution.py:143
  108.0 1.9 copy-start.23
  110.0 1.9 copy-start.13
  111.9 42.1 %copy-start.8 = (bf16[2,1,128,768]{3,2,1,0:T(8,128)(2,1)S(1)}, bf16[2,1,128,768]{3,2,1,0:T(8,128)(2,1)}, u32[]{:S(2)}) copy-start(bf16[2,1,128,768]{3,2,1,0:T(8,128)(2,1)} %param.8) | copy-start | bytes 1179652
  156.0 8.5 %copy-start.5 = (f32[2,128,768]{2,1,0:T(8,128)}, f32[2,128,768]{2,1,0:T(8,128)S(1)}, u32[]{:S(2)}) copy-start(f32[2,128,768]{2,1,0:T(8,128)S(1)} %get-tuple-element.74) | copy-start | bytes 2359300
  156.0 8.5 %copy-start.32 = (f32[2,128]{1,0:T(2,128)}, f32[2,128]{1,0:T(2,128)S(1)}, u32[]{:S(2)}) copy-start(f32[2,128]{1,0:T(2,128)S(1)} %broadcast_multiply_fusion.4) | copy-start | bytes 3076
  156.2 8.3 %copy-start.34 = (f32[2,128]{1,0:T(2,128)}, f32[2,128]{1,0:T(2,128)S(1)}, u32[]{:S(2)}) copy-start(f32[2,128]{1,0:T(2,128)S(1)} %add_rsqrt_fusion) | copy-start | bytes 3076
  156.3 3.2 copy-start.18
  182.0 4.6 copy-start.6
  182.0 4.6 copy-start.19
  182.1 4.6 copy-start.33
  182.1 4.6 copy-start.35
  192.3 3.7 copy-start.12
  192.3 3.7 copy-start.24
  192.3 3.7 copy-start.30
  225.8 9.8 %copy-start.36 = (f32[768]{0:T(1024)S(1)}, f32[768]{0:T(1024)}, u32[]{:S(2)}) copy-start(f32[768]{0:T(1024)} %get-tuple-element.38) | copy-start | bytes 9220
  225.8 9.8 %copy-start.3 = (f32[2,128,768]{2,1,0:T(8,128)S(1)}, f32[2,128,768]{2,1,0:T(8,128)}, u32[]{:S(2)}) copy-start(f32[2,128,768]{2,1,0:T(8,128)} %copy-done.2) | copy-start | bytes 2359300
  225.8 9.8 %copy-start.17 = (bf16[2,12,64,128]{3,2,1,0:T(8,128)(2,1)S(1)}, bf16[2,12,64,128]{3,2,1,0:T(8,128)(2,1)}, u32[]{:S(2)}) copy-start(bf16[2,12,64,128]{3,2,1,0:T(8,128)(2,1)} %convolution_convert_fusion.1) | copy-start | bytes 1179652
  229.1 29.8 %collective-permute-start.3 = (bf16[2,2,64,768]{3,2,1,0:T(8,128)(2,1)}, bf16[2,2,64,768]{3,2,1,0:T(8,128)(2,1)}, u32[]{:S(2)}, u32[]{:S(2)}) collective-permute-start(bf16[2,2,64,768]{3,2,1,0:T(8,128)(2,1)} %get-tuple-element.52), channel_id=1, source_target_pairs={{1,0},{2,1},{3,2},{4,3},{5,4},{6,5},{7,6},{9,8},{10,9},{11,10},{12... | collective-permute-start | bytes 1179656 | tf_op jit(solution)/shard_map/ppermute | solution.py:220
  230.3 28.5 %collective-permute-start.2 = (bf16[2,2,64,768]{3,2,1,0:T(8,128)(2,1)}, bf16[2,2,64,768]{3,2,1,0:T(8,128)(2,1)}, u32[]{:S(2)}, u32[]{:S(2)}) collective-permute-start(bf16[2,2,64,768]{3,2,1,0:T(8,128)(2,1)} %get-tuple-element.51), channel_id=1, source_target_pairs={{0,1},{1,2},{2,3},{3,4},{4,5},{5,6},{6,7},{8,9},{9,10},{10,11},{11... | collective-permute-start | bytes 1179656 | tf_op jit(solution)/shard_map/ppermute | solution.py:219
  263.9 4.1 copy-start.31
  268.1 4.0 copy-start.11
  272.1 10.2 %slice-start = ((s8[10616832]{0:T(1024)(128)(4,1)}), s8[4194304]{0:T(1024)(128)(4,1)S(1)}, s32[]{:S(2)}) async-start(s8[10616832]{0:T(1024)(128)(4,1)} %bitcast.168), calls=%async_computation.4 | async-start | bytes 8388608
  272.1 10.2 %slice-start.1 = ((s8[10616832]{0:T(1024)(128)(4,1)}), s8[4194304]{0:T(1024)(128)(4,1)S(1)}, s32[]{:S(2)}) async-start(s8[10616832]{0:T(1024)(128)(4,1)} %bitcast.168), calls=%async_computation.5 | async-start | bytes 8388608
  275.7 6.6 %copy-start = (f32[768,3200]{1,0:T(8,128)}, f32[768,3200]{1,0:T(8,128)S(1)}, u32[]{:S(2)}) copy-start(f32[768,3200]{1,0:T(8,128)S(1)} %select_maximum_fusion) | copy-start | bytes 29491204
  275.7 6.6 %slice-start.2 = ((s8[10616832]{0:T(1024)(128)(4,1)}), s8[2228224]{0:T(1024)(128)(4,1)S(1)}, s32[]{:S(2)}) async-start(s8[10616832]{0:T(1024)(128)(4,1)} %bitcast.168), calls=%async_computation.6 | async-start | bytes 4456448
  282.3 8.5 %collective-permute-start.4 = (f32[2,192,3200]{2,1,0:T(8,128)}, f32[2,192,3200]{2,1,0:T(8,128)}, u32[]{:S(2)}, u32[]{:S(2)}) collective-permute-start(f32[2,192,3200]{2,1,0:T(8,128)} %dynamic-slice_bitcast_fusion.1), channel_id=1, source_target_pairs={{0,8},{8,0},{16,24},{24,16},{1,9},{9,1},{17,25},{25,17},{2,10},{10... | collective-permute-start | bytes 14745608 | tf_op jit(solution)/shard_map/ppermute | solution.py:31
  285.1 49.1 %collective-permute-start.6 = (f32[2,192,3456]{2,1,0:T(8,128)}, f32[2,192,3456]{2,1,0:T(8,128)}, u32[]{:S(2)}, u32[]{:S(2)}) collective-permute-start(f32[2,192,3456]{2,1,0:T(8,128)} %dynamic-slice_bitcast_fusion), channel_id=1, source_target_pairs={{0,8},{8,0},{16,24},{24,16},{1,9},{9,1},{17,25},{25,17},{2,10},{10... | collective-permute-start | bytes 15925256 | tf_op jit(solution)/shard_map/ppermute | solution.py:31
  295.2 2.3 copy-start.1
  297.6 29.1 %collective-permute-start.5 = (bf16[192,3200]{1,0:T(8,128)(2,1)S(1)}, bf16[192,3200]{1,0:T(8,128)(2,1)S(1)}, u32[]{:S(2)}, u32[]{:S(2)}) collective-permute-start(bf16[192,3200]{1,0:T(8,128)(2,1)S(1)} %fusion.28), channel_id=1, source_target_pairs={{0,16},{8,24},{16,0},{24,8},{1,17},{9,25},{17,1},{25,9},{2,18},{10... | collective-permute-start | bytes 3686408 | tf_op jit(solution)/shard_map/ppermute | solution.py:37
  330.1 59.5 %all-to-all-start = ((f32[8,24,3200]{2,1,0:T(8,128)}), f32[8,24,3200]{2,1,0:T(8,128)S(1)}, u32[]{:S(2)}, u32[]{:S(2)}) async-start(f32[8,24,3200]{2,1,0:T(8,128)} %bitcast.45), calls=%async_computation | async-start | bytes 4915200 | tf_op jit(solution)/shard_map/all_to_all | solution.py:46
  339.0 30.2 %collective-permute-start.7 = (bf16[192,3456]{1,0:T(8,128)(2,1)S(1)}, bf16[192,3456]{1,0:T(8,128)(2,1)S(1)}, u32[]{:S(2)}, u32[]{:S(2)}) collective-permute-start(bf16[192,3456]{1,0:T(8,128)(2,1)S(1)} %fusion.22), channel_id=1, source_target_pairs={{0,16},{8,24},{16,0},{24,8},{1,17},{9,25},{17,1},{25,9},{2,18},{10... | collective-permute-start | bytes 3981320 | tf_op jit(solution)/shard_map/ppermute | solution.py:37
  389.6 1.5 copy-start.10
  391.0 3.8 copy-start.7
  391.0 64.1 %all-to-all-start.1 = ((f32[8,24,3456]{2,1,0:T(8,128)}), f32[8,24,3456]{2,1,0:T(8,128)S(1)}, u32[]{:S(2)}, u32[]{:S(2)}) async-start(f32[8,24,3456]{2,1,0:T(8,128)} %bitcast.173), calls=%async_computation.1 | async-start | bytes 5308416 | tf_op jit(solution)/shard_map/all_to_all | solution.py:46
  394.8 3.3 copy-start.38
  394.8 3.3 copy-start.37
  394.8 3.3 copy-start.4
  394.9 3.3 copy-start.9
  394.9 3.3 copy-start.22
  (6 other events, 4.5 us)
Sparse Core Ops, SparseCore 0:
  11.4 63.4 all-gather.2
  78.3 75.6 all-gather.4

commit v3 on v2

--- a/solution.py
+++ b/solution.py
@@ -18,19 +18,21 @@
 LANES = 128
 
 
-def scatter_sum(value, axes):
-    outer, inner = axes
-    outer_size, inner_size = (lax.axis_size(outer), lax.axis_size(inner))
+def pair_sum(value, outer):
+    outer_size = lax.axis_size(outer)
     pairs = outer_size // 2
-    place = lax.axis_index(outer)
-    core = place % 2
+    core = lax.axis_index(outer) % 2
     blocks = value.reshape(pairs, 2, value.shape[0] // outer_size, value.shape[1])
     other = lax.dynamic_index_in_dim(blocks, 1 - core, axis=1, keepdims=False)
     own = lax.dynamic_index_in_dim(blocks, core, axis=1, keepdims=False)
     swap = [(i, i ^ 1) for i in range(outer_size)]
-    value = own + lax.ppermute(other, outer, swap)
-    if pairs == 2:
-        line = place // 2
+    return own + lax.ppermute(other, outer, swap)
+
+
+def line_sum(value, outer):
+    outer_size = lax.axis_size(outer)
+    if outer_size == 4:
+        line = lax.axis_index(outer) // 2
         other = lax.dynamic_index_in_dim(value, 1 - line, axis=0, keepdims=False)
         own = lax.dynamic_index_in_dim(value, line, axis=0, keepdims=False)
         swap = [(i, i ^ 2) for i in range(outer_size)]
@@ -42,6 +44,11 @@
             value.astype(jnp.bfloat16), outer, 0, 0, axis_index_groups=groups
         )
         value = jnp.sum(arrived.astype(jnp.float32), axis=0)
+    return value
+
+
+def ring_sum(value, inner):
+    inner_size = lax.axis_size(inner)
     blocks = value.reshape(inner_size, value.shape[0] // inner_size, value.shape[1])
     return jnp.sum(lax.all_to_all(blocks, inner, 0, 0), axis=0)
 
@@ -187,13 +194,15 @@
     ffn_grads, d_expanded = lax.optimization_barrier(
         (jnp.concatenate([expand_acc, contract_acc], axis=1), d_expanded)
     )
-    ffn_sum = scatter_sum(ffn_grads, axes)
+    ffn_pair = pair_sum(ffn_grads, "dp")
     d_normed_two = jnp.einsum(
         "bce,de->bcd", d_expanded, full_expand, preferred_element_type=jnp.float32
     )
     d_resid_n, gain_two_part = norm_back(d_normed_two, norm_two, inv_two, full_gain_two)
     d_resid = upstream_half.astype(jnp.float32) + d_resid_n
     d_resid_half = d_resid.astype(jnp.bfloat16)
+    ffn_pair, d_resid_half = lax.optimization_barrier((ffn_pair, d_resid_half))
+    ffn_line = line_sum(ffn_pair, "dp")
     d_attended = jnp.einsum(
         "bce,de->bcd", d_resid_half, full_output, preferred_element_type=jnp.float32
     )
@@ -216,6 +225,8 @@
         ]
     )
     rims = ext_grads.astype(jnp.bfloat16)
+    ffn_line, rims = lax.optimization_barrier((ffn_line, rims))
+    ffn_sum = ring_sum(ffn_line, "seq")
     from_left = lax.ppermute(rims[:, :, group + half :], "seq", up).astype(jnp.float32)
     from_right = lax.ppermute(rims[:, :, :half], "seq", down).astype(jnp.float32)
     d_query = jnp.einsum(
@@ -249,7 +260,8 @@
     gain_parts = jnp.pad(
         jnp.stack([gain_one_part, gain_two_part], axis=1), ((0, 0), (0, LANES - 2))
     )
-    last_sum = scatter_sum(jnp.concatenate([joined_acc, output_acc, gain_parts], axis=1), axes)
+    last_grads = jnp.concatenate([joined_acc, output_acc, gain_parts], axis=1)
+    last_sum = ring_sum(line_sum(pair_sum(last_grads, "dp"), "dp"), "seq")
     return (
         final.astype(jnp.bfloat16).reshape(layer_input.shape),
         input_grad.reshape(layer_input.shape),

time: 465 us -> 447 us (0.961); the launches traced: 464 us -> 439 us
  waiting for transfers between devices: 250 us -> 223 us
    ppermute x4, waiting for transfers between devices: 61.7 us -> 35.5 us  [the longest x2 28.5 us: line_sum(): arrived = lax.ppermute(other.astype(jnp.bfloat16), outer, swap)]
    add x5 -> x4, other arithmetic: 14.4 us -> 13.2 us  [the longest x2 7.52 us: pair_sum(): return own + lax.ppermute(other, outer, swap)]
  transfers between devices with their start and end apart: 12 -> 12, of which waited for: 9 -> 9; matrix products, arithmetic and copies ran while one was open for 15% -> 23% of each run, Pallas kernels for 0% -> 0%
where the time goes in v3:
time: 447 us; the launch traced here: 439 us
  waiting for transfers between devices  223 us (50%)
  matrix products  93.1 us (21%)
  other arithmetic  47.6 us (11%)
  local copies, waits for them, and re-layouts  36.7 us (8%)
  starting transfers between devices  23.3 us (5%)
  between operations  15.1 us (3%)
    all_to_all x2, waiting for transfers between devices, ring_sum(): return jnp.sum(lax.all_to_all(blocks, inner, 0, 0), axis=0)  70.5 us
    all_gather x1, waiting for transfers between devices, per_device(): full_one = lax.all_gather(pack_one, axes, axis=0, tiled=True)  61 us
    all_gather x1, waiting for transfers between devices, per_device(): full_two = lax.all_gather(pack_two, axes, axis=0, tiled=True)  40.6 us
    ppermute x2, waiting for transfers between devices, line_sum(): arrived = lax.ppermute(other.astype(jnp.bfloat16), outer, swap)  28.5 us
    dot_general x1, matrix products, per_device(): jnp.einsum('bhqk,bqhd->bkhd', d_scores, q_rot, preferred_element_type=jnp...  21.4 us
    dot_general x1, matrix products, per_device(): jnp.einsum('bhqk,bkhd->bqhd', d_scores, key_rows, preferred_element_type=...  21.2 us
  transfers between devices with their start and end apart: 12, of which 9 were waited for; matrix products, arithmetic and copies ran while one was open for 23% of the time, Pallas kernels for 0%

profile of v3, /device:TPU:0, one launch (start us, length us, event | category | flops | bytes accessed | tf_op | source)
XLA Modules:
  0.0 438.9 jit_solution(12764800490882718953)
XLA Ops:
  13.9 61.0 %all-gather.3.cloned.1.call-done = bf16[768,2432]{1,0:T(8,128)(2,1)} async-done(((bf16[24,2432]{1,0:T(8,128)(2,1)}), bf16[768,2432]{1,0:T(8,128)(2,1)}) %all-gather.3.cloned.1.call-update) | async-done | bytes 3735568 | tf_op jit(solution)/shard_map/all_gather | solution.py:128
  76.2 3.3 fusion.4
  84.4 4.6 %collective-permute-start = (bf16[2,2,64,768]{3,2,1,0:T(8,128)(2,1)S(1)}, bf16[2,2,64,768]{3,2,1,0:T(8,128)(2,1)S(1)}, u32[]{:S(2)}, u32[]{:S(2)}) collective-permute-start(bf16[2,2,64,768]{3,2,1,0:T(8,128)(2,1)S(1)} %get-tuple-element.71), channel_id=1, source_target_pairs={{0,1},{1,2},{2,3},{3,4},{4,5},{5,6},{6,7},{8,9},{9,10},{10,11},{11... | collective-permute-start | bytes 1179656 | tf_op jit(solution)/shard_map/ppermute | solution.py:150
  89.8 7.9 %collective-permute-done.1 = bf16[2,2,64,768]{3,2,1,0:T(8,128)(2,1)S(1)} collective-permute-done((bf16[2,2,64,768]{3,2,1,0:T(8,128)(2,1)S(1)}, bf16[2,2,64,768]{3,2,1,0:T(8,128)(2,1)S(1)}, u32[]{:S(2)}, u32[]{:S(2)}) %collective-permute-start.1) | collective-permute-done | bytes 393248 | tf_op jit(solution)/shard_map/ppermute | solution.py:151
  97.7 7.7 %collective-permute-done = bf16[2,2,64,768]{3,2,1,0:T(8,128)(2,1)S(1)} collective-permute-done((bf16[2,2,64,768]{3,2,1,0:T(8,128)(2,1)S(1)}, bf16[2,2,64,768]{3,2,1,0:T(8,128)(2,1)S(1)}, u32[]{:S(2)}, u32[]{:S(2)}) %collective-permute-start) | collective-permute-done | bytes 393248 | tf_op jit(solution)/shard_map/ppermute | solution.py:150
  108.1 1.9 fusion.9
  111.9 1.7 convolution_convert_fusion.1
  113.6 40.6 %all-gather.5.cloned.1.call-done = bf16[768,4224]{1,0:T(8,128)(2,1)} async-done(((bf16[24,4224]{1,0:T(8,128)(2,1)}), bf16[768,4224]{1,0:T(8,128)(2,1)}) %all-gather.5.cloned.1.call-update) | async-done | bytes 6488080 | tf_op jit(solution)/shard_map/all_gather | solution.py:129
  154.1 2.0 fusion.103
  156.4 3.2 fusion.6
  159.6 5.3 %multiply_convert_fusion.1 = (bf16[2,128,1152]{2,1,0:T(8,128)(2,1)S(1)}, f32[2,128,1152]{2,1,0:T(8,128)S(1)}, bf16[2,128,1152]{2,1,0:T(8,128)(2,1)S(1)}) fusion(f32[2,128,2304]{2,1,0:T(8,128)S(1)} %fusion.6, bf16[2,1,128,768]{3,2,1,0:T(8,128)(2,1)S(1)} %copy-done.8, bf16[768,4224]{1,0:T(8,128)(2,1)} %all-gather.5.cloned.1.call-done), kind=kOutput, calls=%fused_computation.66 | convolution fusion | flops 475693056 | bytes 6881280 | tf_op jit(solution)/shard_map/bcd,df->bcf/dot_general | solution.py:185
  164.9 4.1 convolution_bitcast_fusion.1
  171.1 2.6 convolution_bitcast_fusion.2
  173.7 8.8 %pad_maximum_fusion = f32[768,3456]{1,0:T(8,128)} fusion(f32[768,1152]{1,0:T(8,128)} %convolution_bitcast_fusion.2, f32[768,2304]{1,0:T(8,128)} %convolution_bitcast_fusion.1), kind=kLoop, calls=%fused_computation.1 | loop fusion | flops 2654208 | bytes 21233664 | tf_op jit(solution)/shard_map/concatenate | solution.py:195
  182.5 5.3 %dynamic-slice_bitcast_fusion = f32[2,192,3456]{2,1,0:T(8,128)} fusion(f32[2,2,192,3456]{3,2,1,0:T(8,128)} %bitcast.173, s32[]{:T(128)S(6)} %select_n.41), kind=kLoop, calls=%fused_computation.7 | loop fusion | bytes 10616836 | tf_op jit(solution)/shard_map/jit(dynamic_index_in_dim)/squeeze | solution.py:26
  188.0 4.0 multiply_reduce_fusion.1
  192.6 1.9 fusion.98
  194.5 2.3 collective-permute-done.2
  196.8 3.1 bitcast_add_fusion
  200.0 2.3 copy-done.4
  205.0 2.5 convolution_convert_fusion
  207.6 1.9 copy.88
  209.5 3.5 fusion.104
  213.0 21.4 %fusion.11 = f32[2,12,64,256]{3,2,1,0:T(8,128)} fusion(f32[2,12,128,256]{3,2,1,0:T(8,128)} %fusion.104, f32[2,12,128,256]{3,2,1,0:T(8,128)S(1)} %get-tuple-element.80, f32[2,12,128]{2,1,0:T(8,128)} %copy-done.27, pred[128,256]{1,0:T(8,128)(4,1)} %fusion.72, bf16[2,128,12,32]{1,3,2,0:T(8,128)(2,1)} %copy-done.20, bf16[2,128,12,32]{1,3,2,0:T(8,128)(2,1)} %copy-done.19), kind=kOutput, calls=%fused_computation.33 | convolution fusion | flops 110103808 | bytes 8302592 | tf_op jit(solution)/shard_map/bhqk,bqhd->bkhd/dot_general | solution.py:215
  234.5 3.2 copy.89
  237.7 3.1 fusion.74
  240.7 3.0 copy.90
  243.8 2.1 fusion.1
  245.9 3.9 bitcast_add_fusion.2
  252.1 5.4 %collective-permute-start.4 = (bf16[2,2,64,768]{3,2,1,0:T(8,128)(2,1)}, bf16[2,2,64,768]{3,2,1,0:T(8,128)(2,1)}, u32[]{:S(2)}, u32[]{:S(2)}) collective-permute-start(bf16[2,2,64,768]{3,2,1,0:T(8,128)(2,1)} %get-tuple-element.59), channel_id=1, source_target_pairs={{0,1},{1,2},{2,3},{3,4},{4,5},{5,6},{6,7},{8,9},{9,10},{10,11},{11... | collective-permute-start | bytes 1179656 | tf_op jit(solution)/shard_map/ppermute | solution.py:230
  257.5 1.9 convolution_bitcast_fusion.4
  259.4 21.2 %fusion.23 = f32[2,128,12,64]{1,3,2,0:T(8,128)} fusion(bf16[2,256,12,64]{1,3,2,0:T(8,128)(2,1)} %bitcast.186, f32[2,12,128,256]{3,2,1,0:T(8,128)} %fusion.104, f32[2,12,128,256]{3,2,1,0:T(8,128)S(1)} %get-tuple-element.80, f32[2,12,128]{2,1,0:T(8,128)} %copy-done.27, pred[128,256]{1,0:T(8,128)(4,1)} %fusion.72), kind=kOutput, calls=%fused_computation.47 | convolution fusion | flops 109317376 | bytes 7909376 | tf_op jit(solution)/shard_map/bhqk,bkhd->bqhd/dot_general | solution.py:232
  280.7 1.7 fusion.18
  285.7 4.2 convolution_bitcast_fusion
  290.0 3.8 fusion.59
  294.0 3.4 select_maximum_fusion
  297.5 2.7 dynamic-slice_bitcast_fusion.1
  300.1 2.5 copy-done.1
  302.7 3.8 all-to-all-start.1
  306.5 4.7 %collective-permute-done.6 = f32[2,192,3200]{2,1,0:T(8,128)} collective-permute-done((f32[2,192,3200]{2,1,0:T(8,128)}, f32[2,192,3200]{2,1,0:T(8,128)}, u32[]{:S(2)}, u32[]{:S(2)}) %collective-permute-start.6) | collective-permute-done | bytes 4915232 | tf_op jit(solution)/shard_map/ppermute | solution.py:29
  311.2 4.4 bitcast_add_fusion.1
  316.4 28.5 %collective-permute-done.7 = bf16[192,3200]{1,0:T(8,128)(2,1)S(1)} collective-permute-done((bf16[192,3200]{1,0:T(8,128)(2,1)S(1)}, bf16[192,3200]{1,0:T(8,128)(2,1)S(1)}, u32[]{:S(2)}, u32[]{:S(2)}) %collective-permute-start.7) | collective-permute-done | bytes 1228832 | tf_op jit(solution)/shard_map/ppermute | solution.py:39
  344.9 1.8 bitcast_add_fusion.3
  346.7 20.7 %all-to-all-done.1 = f32[8,24,3456]{2,1,0:T(8,128)S(1)} async-done(((f32[8,24,3456]{2,1,0:T(8,128)}), f32[8,24,3456]{2,1,0:T(8,128)S(1)}, u32[]{:S(2)}, u32[]{:S(2)}) %all-to-all-start.1) | async-done | bytes 2654240 | tf_op jit(solution)/shard_map/all_to_all | solution.py:53
  367.4 4.5 %all-to-all-start = ((f32[8,24,3200]{2,1,0:T(8,128)}), f32[8,24,3200]{2,1,0:T(8,128)}, u32[]{:S(2)}, u32[]{:S(2)}) async-start(f32[8,24,3200]{2,1,0:T(8,128)} %bitcast.178), calls=%async_computation | async-start | bytes 4915200 | tf_op jit(solution)/shard_map/all_to_all | solution.py:53
  372.0 3.3 fusion.29
  378.2 49.7 %all-to-all-done = f32[8,24,3200]{2,1,0:T(8,128)} async-done(((f32[8,24,3200]{2,1,0:T(8,128)}), f32[8,24,3200]{2,1,0:T(8,128)}, u32[]{:S(2)}, u32[]{:S(2)}) %all-to-all-start) | async-done | bytes 2457632 | tf_op jit(solution)/shard_map/all_to_all | solution.py:53
  428.0 1.8 reduce_sum.138
  (155 shorter events, 35.3 us)
Async XLA Ops:
  7.2 67.7 %all-gather.3.cloned.1.call-start = ((), (), s32[]{:S(2)}) async-start(), calls=%async_computation.2 | async-start | bytes 3852288 | tf_op jit(solution)/shard_map/all_gather | solution.py:128
  9.6 144.6 %all-gather.5.cloned.1.call-start = ((), (), s32[]{:S(2)}) async-start(), calls=%async_computation.3 | async-start | bytes 6690816 | tf_op jit(solution)/shard_map/all_gather | solution.py:129
  13.7 65.8 %copy-start.29 = (f32[2,128]{1,0:T(2,128)}, f32[2,128]{1,0:T(2,128)S(1)}, u32[]{:S(2)}) copy-start(f32[2,128]{1,0:T(2,128)S(1)} %add_rsqrt_fusion.1) | copy-start | bytes 3076
  13.9 67.5 %copy-start.23 = (f32[128,32]{0,1:T(8,128)}, f32[128,32]{0,1:T(8,128)S(1)}, u32[]{:S(2)}) copy-start(f32[128,32]{0,1:T(8,128)S(1)} %get-tuple-element.77) | copy-start | bytes 49156
  13.9 67.5 %copy-start.25 = (f32[128,32]{0,1:T(8,128)}, f32[128,32]{0,1:T(8,128)S(1)}, u32[]{:S(2)}) copy-start(f32[128,32]{0,1:T(8,128)S(1)} %get-tuple-element.78) | copy-start | bytes 49156
  81.6 26.4 %copy-start.19 = (bf16[2,128,12,32]{1,3,2,0:T(8,128)(2,1)}, bf16[2,128,12,32]{1,3,2,0:T(8,128)(2,1)S(1)}, u32[]{:S(2)}) copy-start(bf16[2,128,12,32]{1,3,2,0:T(8,128)(2,1)S(1)} %get-tuple-element.67) | copy-start | bytes 589828
  81.6 26.4 %copy-start.20 = (bf16[2,128,12,32]{1,3,2,0:T(8,128)(2,1)}, bf16[2,128,12,32]{1,3,2,0:T(8,128)(2,1)S(1)}, u32[]{:S(2)}) copy-start(bf16[2,128,12,32]{1,3,2,0:T(8,128)(2,1)S(1)} %get-tuple-element.68) | copy-start | bytes 589828
  83.1 14.6 %collective-permute-start.1 = (bf16[2,2,64,768]{3,2,1,0:T(8,128)(2,1)S(1)}, bf16[2,2,64,768]{3,2,1,0:T(8,128)(2,1)S(1)}, u32[]{:S(2)}, u32[]{:S(2)}) collective-permute-start(bf16[2,2,64,768]{3,2,1,0:T(8,128)(2,1)S(1)} %get-tuple-element.72), channel_id=1, source_target_pairs={{1,0},{2,1},{3,2},{4,3},{5,4},{6,5},{7,6},{9,8},{10,9},{11,10},{12... | collective-permute-start | bytes 1179656 | tf_op jit(solution)/shard_map/ppermute | solution.py:151
  84.4 21.0 %collective-permute-start = (bf16[2,2,64,768]{3,2,1,0:T(8,128)(2,1)S(1)}, bf16[2,2,64,768]{3,2,1,0:T(8,128)(2,1)S(1)}, u32[]{:S(2)}, u32[]{:S(2)}) collective-permute-start(bf16[2,2,64,768]{3,2,1,0:T(8,128)(2,1)S(1)} %get-tuple-element.71), channel_id=1, source_target_pairs={{0,1},{1,2},{2,3},{3,4},{4,5},{5,6},{6,7},{8,9},{9,10},{10,11},{11... | collective-permute-start | bytes 1179656 | tf_op jit(solution)/shard_map/ppermute | solution.py:150
  108.0 1.9 copy-start.22
  110.0 1.9 copy-start.12
  111.9 42.3 %copy-start.5 = (bf16[2,1,128,768]{3,2,1,0:T(8,128)(2,1)S(1)}, bf16[2,1,128,768]{3,2,1,0:T(8,128)(2,1)}, u32[]{:S(2)}) copy-start(bf16[2,1,128,768]{3,2,1,0:T(8,128)(2,1)} %param.8) | copy-start | bytes 1179652
  156.1 8.8 %copy-start.2 = (f32[2,128,768]{2,1,0:T(8,128)}, f32[2,128,768]{2,1,0:T(8,128)S(1)}, u32[]{:S(2)}) copy-start(f32[2,128,768]{2,1,0:T(8,128)S(1)} %get-tuple-element.82) | copy-start | bytes 2359300
  156.4 8.6 %copy-start.33 = (f32[2,128]{1,0:T(2,128)}, f32[2,128]{1,0:T(2,128)S(1)}, u32[]{:S(2)}) copy-start(f32[2,128]{1,0:T(2,128)S(1)} %add_rsqrt_fusion) | copy-start | bytes 3076
  156.4 3.2 copy-start.8
  187.7 9.1 %collective-permute-start.2 = (f32[2,192,3456]{2,1,0:T(8,128)}, f32[2,192,3456]{2,1,0:T(8,128)}, u32[]{:S(2)}, u32[]{:S(2)}) collective-permute-start(f32[2,192,3456]{2,1,0:T(8,128)} %dynamic-slice_bitcast_fusion), channel_id=1, source_target_pairs={{0,8},{8,0},{16,24},{24,16},{1,9},{9,1},{17,25},{25,17},{2,10},{10... | collective-permute-start | bytes 15925256 | tf_op jit(solution)/shard_map/ppermute | solution.py:29
  188.0 8.9 %copy-start = (f32[768,3456]{1,0:T(8,128)S(1)}, f32[768,3456]{1,0:T(8,128)}, u32[]{:S(2)}) copy-start(f32[768,3456]{1,0:T(8,128)} %pad_maximum_fusion) | copy-start | bytes 31850500
  192.0 2.5 copy-start.10
  192.6 7.4 %copy-start.36 = (f32[2,128]{1,0:T(2,128)}, f32[2,128]{1,0:T(2,128)S(1)}, u32[]{:S(2)}) copy-start(f32[2,128]{1,0:T(2,128)S(1)} %broadcast_multiply_fusion.2) | copy-start | bytes 3076
  192.6 7.4 %copy-start.38 = (f32[2,128]{1,0:T(2,128)}, f32[2,128]{1,0:T(2,128)S(1)}, u32[]{:S(2)}) copy-start(f32[2,128]{1,0:T(2,128)S(1)} %broadcast_multiply_fusion.3) | copy-start | bytes 3076
  194.5 10.5 %copy-start.17 = (bf16[2,128,768]{2,1,0:T(8,128)(2,1)}, bf16[2,128,768]{2,1,0:T(8,128)(2,1)S(1)}, u32[]{:S(2)}) copy-start(bf16[2,128,768]{2,1,0:T(8,128)(2,1)S(1)} %fusion.98) | copy-start | bytes 1179652
  200.0 2.4 copy-start.4
  203.6 42.3 %collective-permute-start.3 = (bf16[192,3456]{1,0:T(8,128)(2,1)}, bf16[192,3456]{1,0:T(8,128)(2,1)}, u32[]{:S(2)}, u32[]{:S(2)}) collective-permute-start(bf16[192,3456]{1,0:T(8,128)(2,1)} %fusion.22), channel_id=1, source_target_pairs={{0,16},{8,24},{16,0},{24,8},{1,17},{9,25},{17,1},{25,9},{2,18},{10... | collective-permute-start | bytes 3981320 | tf_op jit(solution)/shard_map/ppermute | solution.py:39
  245.9 11.6 %copy-start.16 = (bf16[2,12,64,128]{3,2,1,0:T(8,128)(2,1)S(1)}, bf16[2,12,64,128]{3,2,1,0:T(8,128)(2,1)}, u32[]{:S(2)}) copy-start(bf16[2,12,64,128]{3,2,1,0:T(8,128)(2,1)} %convolution_convert_fusion.1) | copy-start | bytes 1179652
  245.9 11.6 %copy-start.18 = (bf16[2,128,768]{2,1,0:T(8,128)(2,1)S(1)}, bf16[2,128,768]{2,1,0:T(8,128)(2,1)}, u32[]{:S(2)}) copy-start(bf16[2,128,768]{2,1,0:T(8,128)(2,1)} %copy-done.17) | copy-start | bytes 1179652
  250.9 29.8 %collective-permute-start.5 = (bf16[2,2,64,768]{3,2,1,0:T(8,128)(2,1)}, bf16[2,2,64,768]{3,2,1,0:T(8,128)(2,1)}, u32[]{:S(2)}, u32[]{:S(2)}) collective-permute-start(bf16[2,2,64,768]{3,2,1,0:T(8,128)(2,1)} %get-tuple-element.60), channel_id=1, source_target_pairs={{1,0},{2,1},{3,2},{4,3},{5,4},{6,5},{7,6},{9,8},{10,9},{11,10},{12... | collective-permute-start | bytes 1179656 | tf_op jit(solution)/shard_map/ppermute | solution.py:231
  252.1 28.5 %collective-permute-start.4 = (bf16[2,2,64,768]{3,2,1,0:T(8,128)(2,1)}, bf16[2,2,64,768]{3,2,1,0:T(8,128)(2,1)}, u32[]{:S(2)}, u32[]{:S(2)}) collective-permute-start(bf16[2,2,64,768]{3,2,1,0:T(8,128)(2,1)} %get-tuple-element.59), channel_id=1, source_target_pairs={{0,1},{1,2},{2,3},{3,4},{4,5},{5,6},{6,7},{8,9},{9,10},{10,11},{11... | collective-permute-start | bytes 1179656 | tf_op jit(solution)/shard_map/ppermute | solution.py:230
  283.2 2.6 copy-start.30
  285.7 4.2 copy-start.28
  285.7 4.2 copy-start.31
  290.0 3.8 copy-start.35
  290.0 4.0 copy-start.7
  297.4 5.2 %copy-start.1 = (f32[768,3200]{1,0:T(8,128)}, f32[768,3200]{1,0:T(8,128)S(1)}, u32[]{:S(2)}) copy-start(f32[768,3200]{1,0:T(8,128)S(1)} %select_maximum_fusion) | copy-start | bytes 29491204
  302.7 8.5 %collective-permute-start.6 = (f32[2,192,3200]{2,1,0:T(8,128)}, f32[2,192,3200]{2,1,0:T(8,128)}, u32[]{:S(2)}, u32[]{:S(2)}) collective-permute-start(f32[2,192,3200]{2,1,0:T(8,128)} %dynamic-slice_bitcast_fusion.1), channel_id=1, source_target_pairs={{0,8},{8,0},{16,24},{24,16},{1,9},{9,1},{17,25},{25,17},{2,10},{10... | collective-permute-start | bytes 14745608 | tf_op jit(solution)/shard_map/ppermute | solution.py:29
  302.7 64.7 %all-to-all-start.1 = ((f32[8,24,3456]{2,1,0:T(8,128)}), f32[8,24,3456]{2,1,0:T(8,128)S(1)}, u32[]{:S(2)}, u32[]{:S(2)}) async-start(f32[8,24,3456]{2,1,0:T(8,128)} %bitcast.177), calls=%async_computation.1 | async-start | bytes 5308416 | tf_op jit(solution)/shard_map/all_to_all | solution.py:53
  315.7 29.1 %collective-permute-start.7 = (bf16[192,3200]{1,0:T(8,128)(2,1)S(1)}, bf16[192,3200]{1,0:T(8,128)(2,1)S(1)}, u32[]{:S(2)}, u32[]{:S(2)}) collective-permute-start(bf16[192,3200]{1,0:T(8,128)(2,1)S(1)} %fusion.28), channel_id=1, source_target_pairs={{0,16},{8,24},{16,0},{24,8},{1,17},{9,25},{17,1},{25,9},{2,18},{10... | collective-permute-start | bytes 3686408 | tf_op jit(solution)/shard_map/ppermute | solution.py:39
  367.4 4.5 %copy-start.3 = (f32[2,128,768]{2,1,0:T(8,128)S(1)}, f32[2,128,768]{2,1,0:T(8,128)}, u32[]{:S(2)}) copy-start(f32[2,128,768]{2,1,0:T(8,128)} %copy-done.2) | copy-start | bytes 2359300
  367.4 60.6 %all-to-all-start = ((f32[8,24,3200]{2,1,0:T(8,128)}), f32[8,24,3200]{2,1,0:T(8,128)}, u32[]{:S(2)}, u32[]{:S(2)}) async-start(f32[8,24,3200]{2,1,0:T(8,128)} %bitcast.178), calls=%async_computation | async-start | bytes 4915200 | tf_op jit(solution)/shard_map/all_to_all | solution.py:53
  371.9 3.4 copy-start.41
  371.9 3.4 copy-start.40
  371.9 3.4 copy-start.6
  372.0 3.4 copy-start.9
  372.0 3.4 copy-start.11
  372.0 3.4 copy-start.21
  372.0 3.4 copy-start.32
  372.0 3.4 copy-start.34
  372.0 3.4 copy-start.37
  372.0 3.4 copy-start.39
  (6 other events, 5.0 us)
Sparse Core Ops, SparseCore 0:
  11.4 63.4 all-gather.2
  78.3 75.7 all-gather.4
